TPU v7x, 32 devices: a whole 2x2x4 slice. The times are simulated.
32 devices in a mesh: groups: 2 (over y), ctx: 16 (over z, x, core).
Axes of the slice: x: 2, y: 2, z: 4, core: 2. Of those that a mesh axis runs over, the one named last changes fastest.
Arguments:
- x_in: bfloat16 [4096, 8192], P(('groups', 'ctx')), parts along dimension 0, may hold values from -6 to 6
- bc_in: bfloat16 [4096, 2048], P(('groups', 'ctx')), parts along dimension 0, may hold values from -6 to 6
- z_in: bfloat16 [4096, 8192], P(('groups', 'ctx')), parts along dimension 0, may hold values from -6 to 6
- dt_in: bfloat16 [4096, 128], P(('groups', 'ctx')), parts along dimension 0, may hold values from -4 to 4
- conv_x: float32 [4, 8192], replicated, may hold values from -3 to 3
- conv_bc: float32 [4, 2048], replicated, may hold values from -3 to 3
- dt_bias: float32 [128], replicated, may hold values from -6 to -3
- a_rate: float32 [128], replicated, may hold values from 0.001953125 to 1
- d_skip: float32 [128], replicated, may hold values from 0.5 to 2
- gain: float32 [8192], replicated, may hold values from 0.5 to 1.5
Outputs:
- mixed: bfloat16 [4096, 8192], P(('groups', 'ctx')), parts along dimension 0
There are 2 independent parts, one for each index of `groups`. A program takes and returns all parts, laid end to end along the dimension named above; an argument that names none is the same for every part. Nothing has to cross between parts.
All inputs are finite; a program needn't handle non-finite values.
Results may differ from a plain program's by a relative error of at most 0.001.
Values may be sent and summed in bfloat16 or wider, within the bound.
No kernel may reach another device: no remote copies, remote signals or barrier semaphores. Data moves between devices by JAX's collectives and lax.ppermute only.
A program may use at most 64 MiB of HBM per device.

v0:
```python
import jax
import jax.numpy as jnp
from jax import lax
from jax.sharding import PartitionSpec as P

STATE = 128
GROUPS = 8


HIGH = lax.Precision.HIGHEST


def shifted(array, axis, by):
    size = lax.axis_size(axis)
    pairs = [(i, i + by) for i in range(size) if 0 <= i + by < size]
    return lax.ppermute(array, axis, pairs)


def block_terms(xc, bcc, dt, a_rate, n_groups, n_state):
    rows, width = xc.shape
    heads = dt.shape[1]
    per = heads // n_groups
    hdim = width // heads
    bmat = bcc[:, : n_groups * n_state].reshape(rows, n_groups, n_state)
    cmat = bcc[:, n_groups * n_state :].reshape(rows, n_groups, n_state)
    cumg = jnp.cumsum(-dt * a_rate, axis=0).reshape(rows, n_groups, per)
    dtg = dt.reshape(rows, n_groups, per)
    xg = xc.reshape(rows, n_groups, per, hdim)
    scores = jnp.einsum("tgn,sgn->gts", cmat, bmat, precision=HIGH)
    cum_t = jnp.transpose(cumg, (1, 2, 0))
    diff = cum_t[:, :, :, None] - cum_t[:, :, None, :]
    posit = jnp.arange(rows)
    causal = posit[:, None] >= posit[None, :]
    decay = jnp.exp(jnp.where(causal[None, None], diff, -jnp.inf))
    dt_t = jnp.transpose(dtg, (1, 2, 0))
    weights = scores[:, None] * decay * dt_t[:, :, None, :]
    y_diag = jnp.einsum("gkts,sgkp->tgkp", weights, xg, precision=HIGH)
    tail = jnp.exp(cumg[-1] - cumg) * dtg
    s_loc = jnp.einsum("sgkp,sgn->gkpn", xg * tail[..., None], bmat, precision=HIGH)
    total = jnp.exp(cumg[-1])
    return (y_diag, s_loc, total, jnp.exp(cumg), cmat, xg)


def join_rows(earlier, later):
    return (earlier[0] * later[0], later[0][..., None] * earlier[1] + later[1])


def shards(x_in, bc_in, z_in, dt_in, conv_x, conv_bc, dt_bias, a_rate, d_skip, gain):
    rows, width = x_in.shape
    heads = dt_bias.shape[0]
    hdim = width // heads
    per = heads // GROUPS
    taps_count = conv_x.shape[0]
    joined = jnp.concatenate([x_in, bc_in], axis=1)
    rim = shifted(joined[rows - (taps_count - 1) :], "ctx", 1)
    extended = jnp.concatenate([rim, joined], axis=0).astype(jnp.float32)
    taps = jnp.concatenate([conv_x, conv_bc], axis=1)
    mixed_in = taps[0] * extended[0:rows]
    for k in range(1, taps_count):
        mixed_in = mixed_in + taps[k] * extended[k : k + rows]
    conv = jax.nn.silu(mixed_in)
    xc = conv[:, :width]
    bcc = conv[:, width:]
    dt = jax.nn.softplus(dt_in.astype(jnp.float32) + dt_bias)
    y_diag, s_loc, total, ecum, cmat, xg = block_terms(xc, bcc, dt, a_rate, GROUPS, STATE)
    flat = s_loc.reshape(1, heads * hdim, STATE)
    spread_decay = jnp.broadcast_to(total[:, :, None], (GROUPS, per, hdim)).reshape(1, heads * hdim)
    decays_all, states_all = (
        lax.all_to_all(spread_decay, "ctx", split_axis=1, concat_axis=0, tiled=True),
        lax.all_to_all(flat, "ctx", split_axis=1, concat_axis=0, tiled=True),
    )
    running = lax.associative_scan(join_rows, (decays_all, states_all), axis=0)[1]
    before = jnp.concatenate([jnp.zeros_like(running[:1]), running[:-1]], axis=0)
    back = lax.all_to_all(before, "ctx", split_axis=0, concat_axis=1, tiled=True)
    s_in = back.reshape(GROUPS, per, hdim, STATE)
    y_off = jnp.einsum("tgn,gkpn->tgkp", cmat, s_in, precision=HIGH) * ecum[..., None]
    dskip = d_skip.reshape(GROUPS, per)[None, :, :, None] * xg
    y = (y_diag + y_off + dskip).reshape(rows, width)
    gated = y * jax.nn.silu(z_in.astype(jnp.float32))
    grouped = gated.reshape(rows, GROUPS, per * hdim)
    scale = lax.rsqrt(jnp.mean(grouped * grouped, axis=-1, keepdims=True) + 1e-05)
    return ((grouped * scale).reshape(rows, width) * gain).astype(jnp.bfloat16)


def solution(mesh):
    return jax.shard_map(
        shards,
        mesh=mesh,
        in_specs=(
            P(("groups", "ctx"), None),
            P(("groups", "ctx"), None),
            P(("groups", "ctx"), None),
            P(("groups", "ctx"), None),
            P(),
            P(),
            P(),
            P(),
            P(),
            P(),
        ),
        out_specs=P(("groups", "ctx"), None),
        check_vma=False,
    )
```

profile of v0, /device:TPU:11, one launch (start us, length us, event | category | flops | bytes accessed | tf_op | source)
XLA Modules:
  0.0 350.5 jit_solution(4362788751913986516)
XLA Ops:
  2.9 6.5 %all-to-all-start.1 = ((f32[1,16,512]{2,0,1:T(1,128)}), f32[1,16,512]{2,0,1:T(1,128)S(1)}, u32[]{:S(2)}, u32[]{:S(2)}) async-start(f32[1,16,512]{2,0,1:T(1,128)} %all_to_all.32), calls=%async_computation.1 | async-start | bytes 65536 | tf_op jit(solution)/shard_map/all_to_all | solution.py:69
  10.7 3.2 copy.54
  14.0 7.7 %pad_maximum_fusion = bf16[3,10240]{0,1:T(8,128)(2,1)} fusion(bf16[128,2048]{0,1:T(8,128)(2,1)S(1)} %copy.55, bf16[128,8192]{0,1:T(8,128)(2,1)S(1)} %copy.54), kind=kLoop, calls=%fused_computation.33 | loop fusion | flops 122880 | bytes 2682880 | tf_op jit(solution)/shard_map/concatenate | solution.py:54
  23.9 3.5 %collective-permute-start = (bf16[3,10240]{1,0:T(4,128)(2,1)S(1)}, bf16[3,10240]{1,0:T(4,128)(2,1)S(1)}, u32[]{:S(2)}, u32[]{:S(2)}) collective-permute-start(bf16[3,10240]{1,0:T(4,128)(2,1)S(1)} %copy.56), channel_id=1, source_target_pairs={{0,1},{1,2},{2,3},{3,4},{4,5},{5,6},{6,7},{7,8},{8,9},{9,10},{10,1... | collective-permute-start | bytes 184328 | tf_op jit(solution)/shard_map/ppermute | solution.py:16
  30.8 9.3 %maximum_convert_fusion = f32[131,10240]{0,1:T(8,128)S(1)} fusion(bf16[128,2048]{0,1:T(8,128)(2,1)S(1)} %copy.55, bf16[128,8192]{0,1:T(8,128)(2,1)S(1)} %copy.54, bf16[3,10240]{0,1:T(8,128)(2,1)} %copy.57), kind=kLoop, calls=%fused_computation.15 | loop fusion | flops 8048640 | bytes 8048640 | tf_op jit(solution)/shard_map/convert_element_type | solution.py:56
  40.1 11.2 %divide_multiply_fusion = f32[128,10240]{0,1:T(8,128)S(1)} fusion(f32[131,10240]{0,1:T(8,128)S(1)} %maximum_convert_fusion, f32[10240]{0:T(1024)S(1)} %bitcast.73, f32[10240]{0:T(1024)S(1)} %bitcast.74, f32[10240]{0:T(1024)S(1)} %bitcast.75, f32[10240]{0:T(1024)S(1)} %bitcast.72), kind=kLoop, calls=%fused_computation.16 | loop fusion | flops 14417920 | bytes 26378240 | tf_op jit(solution)/shard_map/jit(silu)/mul | solution.py:61
  54.5 5.3 %fusion.15 = f32[8,16,64,128]{3,2,1,0:T(8,128)} fusion(f32[128,8,128,1]{0,2,3,1:T(8,128)S(1)} %bitcast.62, f32[128,8,16,64]{0,3,2,1:T(8,128)S(1)} %bitcast.54, f32[128,8,16]{0,2,1:T(8,128)S(1)} %get-tuple-element.16), kind=kOutput, calls=%fused_computation.25 | convolution fusion | flops 1611661312 | bytes 8978432 | tf_op jit(solution)/shard_map/sgkp,sgn->gkpn/dot_general | solution.py:39
  59.8 6.9 %all-to-all-start = ((f32[1,8192,128]{2,0,1:T(1,128)}), f32[1,8192,128]{2,0,1:T(1,128)}, u32[]{:S(2)}, u32[]{:S(2)}) async-start(f32[1,8192,128]{2,0,1:T(1,128)} %bitcast.56), calls=%async_computation | async-start | bytes 8388608 | tf_op jit(solution)/shard_map/all_to_all | solution.py:70
  67.6 91.7 %all-to-all-done = f32[1,8192,128]{2,0,1:T(1,128)} async-done(((f32[1,8192,128]{2,0,1:T(1,128)}), f32[1,8192,128]{2,0,1:T(1,128)}, u32[]{:S(2)}, u32[]{:S(2)}) %all-to-all-start) | async-done | bytes 4194336 | tf_op jit(solution)/shard_map/all_to_all | solution.py:70
  167.1 2.7 pad.29
  176.8 2.8 pad.31
  179.6 3.3 add.112
  186.2 7.6 %pad.48 = f32[15,512,128]{2,1,0:T(8,128)} pad(f32[8,512,128]{2,1,0:T(8,128)} %pad_maximum_fusion.1, f32[]{:T(128)} %constant.9.clone.1), padding=0_0_1x0_0_0x0_0_0 | pad | bytes 6029316 | tf_op jit(solution)/shard_map/slice | solution.py:73
  193.8 5.1 %pad.73 = f32[16,512,128]{2,1,0:T(8,128)} pad(f32[8,512,128]{2,1,0:T(8,128)S(1)} %copy-done.4, f32[]{:T(128)} %constant.9.clone.1), padding=1_0_1x0_0_0x0_0_0 | pad | bytes 6291460
  198.9 3.7 %slice_add_fusion.4 = f32[15,512,128]{2,1,0:T(8,128)S(1)} fusion(f32[15,512,128]{2,1,0:T(8,128)} %pad.48, f32[16,512,128]{2,1,0:T(8,128)} %pad.73), kind=kLoop, calls=%fused_computation.70 | loop fusion | flops 983040 | bytes 11796480 | tf_op jit(solution)/shard_map/add | solution.py:72
  205.1 5.3 %all-to-all-start.2 = ((f32[16,512,128]{2,1,0:T(8,128)}), f32[16,512,128]{2,1,0:T(8,128)}, u32[]{:S(2)}, u32[]{:S(2)}) async-start(f32[16,512,128]{2,1,0:T(8,128)} %concatenate.27), calls=%async_computation.2 | async-start | bytes 8388608 | tf_op jit(solution)/shard_map/all_to_all | solution.py:74
  211.6 91.2 %all-to-all-done.2 = f32[16,512,128]{2,1,0:T(8,128)} async-done(((f32[16,512,128]{2,1,0:T(8,128)}), f32[16,512,128]{2,1,0:T(8,128)}, u32[]{:S(2)}, u32[]{:S(2)}) %all-to-all-start.2) | async-done | bytes 4194336 | tf_op jit(solution)/shard_map/all_to_all | solution.py:74
  302.7 5.6 %fusion.39 = f32[8,16,64,128]{3,2,1,0:T(8,128)S(1)} fusion(f32[8,16,64,128]{3,2,1,0:T(8,128)} %bitcast.21, f32[128,8,128,1]{0,2,3,1:T(8,128)S(1)} %bitcast.61), kind=kOutput, calls=%fused_computation.72 | convolution fusion | flops 1610612736 | bytes 8912896 | tf_op jit(solution)/shard_map/tgn,gkpn->tgkp/dot_general | solution.py:76
  308.4 18.1 %fusion.14 = f32[128,8,16,64]{0,3,2,1:T(8,128)} fusion(f32[8,16,64,128]{3,2,1,0:T(8,128)S(1)} %fusion.39, f32[128,8,16,64]{0,3,2,1:T(8,128)S(1)} %bitcast.55, f32[8,16,128]{2,1,0:T(8,128)S(1)} %bitcast.66, f32[8,16,128]{2,1,0:T(8,128)S(1)} %bitcast.68, f32[8,128,128]{2,1,0:T(8,128)S(1)} %fusion.38, pred[128,128]{1,0:T(8,128)(4,1)S(1)} %iota_compare_fusion, ...), kind=kOutput, calls=%fused_computation.23 | convolution fusion | flops 1623195648 | bytes 13320704 | tf_op jit(solution)/shard_map/gkts,sgkp->tgkp/dot_general | solution.py:37
  326.4 6.0 %copy.66 = f32[128,8192]{1,0:T(8,128)} copy(f32[128,8192]{0,1:T(8,128)} %bitcast.64) | data formatting | bytes 8388608 | tf_op jit(solution)/shard_map/reshape | solution.py:78
  332.4 3.3 fusion.32
  335.8 5.2 %copy.78 = f32[16,8,8,1024]{3,2,1,0:T(8,128)} copy(f32[16,8,8,1024]{3,1,2,0:T(8,128)S(1)} %bitcast.59) | data formatting | bytes 8388608
  344.0 3.3 copy.79
  347.3 2.7 multiply_convert_fusion
  (91 shorter events, 38.3 us)
Async XLA Ops:
  2.9 57.0 %all-to-all-start.1 = ((f32[1,16,512]{2,0,1:T(1,128)}), f32[1,16,512]{2,0,1:T(1,128)S(1)}, u32[]{:S(2)}, u32[]{:S(2)}) async-start(f32[1,16,512]{2,0,1:T(1,128)} %all_to_all.32), calls=%async_computation.1 | async-start | bytes 65536 | tf_op jit(solution)/shard_map/all_to_all | solution.py:69
  13.9 13.6 %copy-start.11 = (f32[4,8192]{1,0:T(4,128)S(1)}, f32[4,8192]{1,0:T(4,128)}, u32[]{:S(2)}) copy-start(f32[4,8192]{1,0:T(4,128)} %param.14) | copy-start | bytes 393220
  13.9 13.6 %copy-start.14 = (f32[4,2048]{1,0:T(4,128)S(1)}, f32[4,2048]{1,0:T(4,128)}, u32[]{:S(2)}) copy-start(f32[4,2048]{1,0:T(4,128)} %param.15) | copy-start | bytes 98308
  23.9 4.8 %collective-permute-start = (bf16[3,10240]{1,0:T(4,128)(2,1)S(1)}, bf16[3,10240]{1,0:T(4,128)(2,1)S(1)}, u32[]{:S(2)}, u32[]{:S(2)}) collective-permute-start(bf16[3,10240]{1,0:T(4,128)(2,1)S(1)} %copy.56), channel_id=1, source_target_pairs={{0,1},{1,2},{2,3},{3,4},{4,5},{5,6},{6,7},{7,8},{8,9},{9,10},{10,1... | collective-permute-start | bytes 184328 | tf_op jit(solution)/shard_map/ppermute | solution.py:16
  52.2 0.8 copy-start.7
  52.5 1.9 copy-start.2
  59.8 99.4 %all-to-all-start = ((f32[1,8192,128]{2,0,1:T(1,128)}), f32[1,8192,128]{2,0,1:T(1,128)}, u32[]{:S(2)}, u32[]{:S(2)}) async-start(f32[1,8192,128]{2,0,1:T(1,128)} %bitcast.56), calls=%async_computation | async-start | bytes 8388608 | tf_op jit(solution)/shard_map/all_to_all | solution.py:70
  169.8 3.8 %copy-start.10 = (f32[1,512,128]{2,1,0:T(8,128)S(1)}, f32[1,512,128]{2,1,0:T(8,128)}, u32[]{:S(2)}) copy-start(f32[1,512,128]{2,1,0:T(8,128)} %slice.192) | copy-start | bytes 786436
  173.6 3.2 copy-start.9
  179.6 3.3 copy-start.1
  184.7 9.0 %copy-start.4 = (f32[8,512,128]{2,1,0:T(8,128)S(1)}, f32[8,512,128]{2,1,0:T(8,128)}, u32[]{:S(2)}) copy-start(f32[8,512,128]{2,1,0:T(8,128)} %add.112) | copy-start | bytes 6291460
  205.1 5.3 %copy-start.15 = (f32[128]{0:T(128)S(1)}, f32[128]{0:T(128)}, u32[]{:S(2)}) copy-start(f32[128]{0:T(128)} %param.18) | copy-start | bytes 1540
  205.1 5.4 %copy-start.6 = (f32[128,1024]{0,1:T(8,128)S(1)}, f32[128,1024]{0,1:T(8,128)}, u32[]{:S(2)}) copy-start(f32[128,1024]{0,1:T(8,128)} %get-tuple-element.5) | copy-start | bytes 1572868
  205.1 5.4 %copy-start.8 = (f32[128,1024]{0,1:T(8,128)S(1)}, f32[128,1024]{0,1:T(8,128)}, u32[]{:S(2)}) copy-start(f32[128,1024]{0,1:T(8,128)} %copy-done.7) | copy-start | bytes 1572868
  205.1 97.6 %all-to-all-start.2 = ((f32[16,512,128]{2,1,0:T(8,128)}), f32[16,512,128]{2,1,0:T(8,128)}, u32[]{:S(2)}, u32[]{:S(2)}) async-start(f32[16,512,128]{2,1,0:T(8,128)} %concatenate.27), calls=%async_computation.2 | async-start | bytes 8388608 | tf_op jit(solution)/shard_map/all_to_all | solution.py:74
  302.7 5.6 %copy-start.3 = (f32[128,8192]{0,1:T(8,128)S(1)}, f32[128,8192]{0,1:T(8,128)}, u32[]{:S(2)}) copy-start(f32[128,8192]{0,1:T(8,128)} %copy-done.2) | copy-start | bytes 12582916
  302.7 5.6 %copy-start.12 = (f32[128,8,16]{0,2,1:T(8,128)S(1)}, f32[128,8,16]{0,2,1:T(8,128)}, u32[]{:S(2)}) copy-start(f32[128,8,16]{0,2,1:T(8,128)} %get-tuple-element.15) | copy-start | bytes 196612
  326.4 6.0 %copy-start.5 = (bf16[128,8192]{1,0:T(8,128)(2,1)S(1)}, bf16[128,8192]{1,0:T(8,128)(2,1)}, u32[]{:S(2)}) copy-start(bf16[128,8192]{1,0:T(8,128)(2,1)} %param.12) | copy-start | bytes 6291460
  344.0 3.3 copy-start
  344.0 3.3 copy-start.13
where the time goes:
time: 355 us; the launch traced here: 350 us
  waiting for transfers between devices  183 us (52%)
  other arithmetic  58.5 us (16%)
  local copies, waits for them, and re-layouts  55.6 us (16%)
  matrix products  30.1 us (8%)
  starting transfers between devices  22.3 us (6%)
    all_to_all x1, waiting for transfers between devices, shards(): lax.all_to_all(flat, 'ctx', split_axis=1, concat_axis=0, tiled=True)  91.7 us
    all_to_all x1, waiting for transfers between devices, shards(): lax.all_to_all(before, 'ctx', split_axis=0, concat_axis=1, tiled=True)  91.2 us
    unnamed x40, local copies, waits for them, and re-layouts  21 us
    dot_general x1, matrix products, block_terms(): y_diag = jnp.einsum('gkts,sgkp->tgkp', weights, xg, precision=HIGH)  18.1 us
    mul x1, other arithmetic, shards(): conv = jax.nn.silu(mixed_in)  11.2 us
    add x4, other arithmetic, shards(): lax.associative_scan(join_rows, (decays_all, states_all), axis=0)[1]  10.2 us
    convert_element_type x1, other arithmetic, shards(): extended = jnp.concatenate([rim, joined], axis=0).astype(jnp.float32)  9.3 us
    pad x4, local copies, waits for them, and re-layouts, shards(): lax.associative_scan(join_rows, (decays_all, states_all), axis=0)[1]  8.84 us
  transfers between devices with their start and end apart: 4, of which 3 were waited for; matrix products, arithmetic and copies ran while one was open for 13% of the time, Pallas kernels for 0%

commit v1 on v0

v1 whole, which is shorter than its diff:
```python
import functools

import jax
import jax.numpy as jnp
from jax import lax
from jax.experimental import pallas as pl
from jax.experimental.pallas import tpu as pltpu
from jax.sharding import PartitionSpec as P

STATE = 128
GROUPS = 8
EPS = 1e-05
F32, BF16 = jnp.float32, jnp.bfloat16
WIRE = jnp.float16
PEAK = 4 * 3.0 * 6.0
DT_TOP = 1.3133


def plane_size(n, groups):
    size = 1
    while (2 * size) ** 3 <= 4 * n and n % (2 * size) == 0 and groups % (2 * size) == 0:
        size *= 2
    return size


def silu(v):
    return v / (1.0 + jnp.exp(-v))


def split(v):
    hi = v.astype(BF16)
    return hi, (v - hi.astype(F32)).astype(BF16)


def mm(a, b, dims=((1,), (0,))):
    return lax.dot_general(a, b, (dims, ((), ())), preferred_element_type=F32)


def spread(v, e_ref):
    hi = v.astype(BF16)
    rest = v - hi.astype(F32)
    mid = rest.astype(BF16)
    low = (rest - mid.astype(F32)).astype(BF16)
    return mm(jnp.concatenate([hi, mid, low], axis=1), e_ref[...])


def conv_silu(x, halo, taps):
    rows = x.shape[0]
    count = taps.shape[0]
    xf = x.astype(F32)
    hf = halo.astype(F32)
    at = lax.broadcasted_iota(jnp.int32, (rows, 1), 0)
    total = taps[count - 1 : count] * xf
    for back in range(1, count):
        moved = pltpu.roll(xf, back, 0)
        for row in range(back):
            src = hf.shape[0] - back + row
            moved = jnp.where(at == row, hf[src : src + 1], moved)
        total = total + taps[count - 1 - back : count - back] * moved
    return silu(total)


def steps_kernel(dt_ref, bias_ref, rate_ref, skip_ref, tail_ref, cum_ref, row_ref, ecum_ref, tot_ref):
    groups, rows, per = tail_ref.shape
    v = dt_ref[...].astype(F32) + bias_ref[...]
    dt = jnp.maximum(v, 0.0) + jnp.log1p(jnp.exp(-jnp.abs(v)))
    cum = -rate_ref[...] * dt
    at = lax.broadcasted_iota(jnp.int32, cum.shape, 0)
    step = 1
    while step < rows:
        cum = cum + jnp.where(at >= step, pltpu.roll(cum, step, 0), 0.0)
        step *= 2
    total = cum[rows - 1 : rows]
    tot_ref[...] = total
    tail = jnp.exp(total - cum) * dt
    ecum = jnp.exp(cum)
    row = (jnp.log(dt) - cum).T
    for g in range(groups):
        cols = slice(g * per, (g + 1) * per)
        tail_ref[g] = tail[:, cols]
        cum_ref[g] = cum[:, cols]
        row_ref[g] = row[cols]
        ecum_ref[g, :rows] = ecum[:, cols]
        ecum_ref[g, rows:] = jnp.broadcast_to(skip_ref[:, cols], (8, per))


def state_kernel(order_ref, x_ref, xh_ref, tx_ref, b_ref, bh_ref, tb_ref, tail_ref, e_ref, s_ref, xc_ref):
    xc = conv_silu(x_ref[...], xh_ref[...], tx_ref[...])
    xc_ref[0] = xc
    b = conv_silu(b_ref[...], bh_ref[...], tb_ref[...])
    xt = xc * spread(tail_ref[0], e_ref)
    xhi, xlo = split(xt)
    bhi, blo = split(b)
    s = mm(jnp.concatenate([bhi, blo], axis=0), jnp.concatenate([xhi, xhi], axis=0), ((0,), (0,)))
    s_ref[0] = s + mm(bhi, xlo, ((0,), (0,)))


def local_kernel(order_ref, b_ref, bh_ref, tb_ref, c_ref, ch_ref, tc_ref, xc_ref, cum_ref, row_ref, ecum_ref, e_ref, z_ref, m1_ref, m2_ref, co_ref):
    rows = z_ref.shape[0]
    per = cum_ref.shape[2]
    hdim = z_ref.shape[1] // per
    b = conv_silu(b_ref[...], bh_ref[...], tb_ref[...])
    c = conv_silu(c_ref[...], ch_ref[...], tc_ref[...])
    co_ref[0] = c
    bhi, blo = split(b)
    chi, clo = split(c)
    last = ((1,), (1,))
    scores = mm(jnp.concatenate([chi, clo], axis=1), jnp.concatenate([bhi, bhi], axis=1), last) + mm(chi, blo, last)
    causal = lax.broadcasted_iota(jnp.int32, (rows, rows), 0) >= lax.broadcasted_iota(jnp.int32, (rows, rows), 1)
    wide = spread(ecum_ref[0], e_ref)
    z = silu(z_ref[...].astype(F32))
    m1_ref[0] = wide[:rows] * z
    skip = wide[rows : rows + 1]
    first = lax.broadcasted_iota(jnp.int32, (rows, 2 * hdim), 1) < hdim
    for pair in range(per // 2):
        cols = slice(pair * 2 * hdim, (pair + 1) * 2 * hdim)
        weights = []
        for h in (2 * pair, 2 * pair + 1):
            e = jnp.exp(cum_ref[0, :, h : h + 1] + row_ref[0, h : h + 1, :])
            weights.append(jnp.where(causal, e * scores, 0.0))
        w = jnp.concatenate(weights, axis=1)
        x = xc_ref[0, :, cols]
        xb = jnp.concatenate([jnp.where(first, x, 0.0), jnp.where(first, 0.0, x)], axis=0)
        whi, wlo = split(w)
        xhi, xlo = split(xb)
        y = mm(whi, xhi) + mm(wlo, xhi) + mm(whi, xlo)
        m2_ref[0, :, cols] = (y + skip[:, cols] * x) * z[:, cols]


def finish_kernel(order_ref, p_ref, c_ref, m1_ref, m2_ref, gain_ref, held_ref, out_ref):
    chi, clo = split(c_ref[0])
    phi, plo = split(p_ref[0])
    y = mm(jnp.concatenate([chi, clo], axis=1), jnp.concatenate([phi, phi], axis=0)) + mm(chi, plo)
    gated = m2_ref[0] + m1_ref[0] * y
    scale = lax.rsqrt(jnp.mean(gated * gated, axis=1, keepdims=True) + EPS)
    out_ref[...] = (gated * scale * gain_ref[...]).astype(BF16)


def call(body, order, out_shape, in_specs, out_specs, args, **more):
    grid_spec = pltpu.PrefetchScalarGridSpec(
        num_scalar_prefetch=1, grid=order.shape, in_specs=in_specs, out_specs=out_specs
    )
    return pl.pallas_call(body, out_shape=out_shape, grid_spec=grid_spec, **more)(order, *args)


def shards(x_in, bc_in, z_in, dt_in, conv_x, conv_bc, dt_bias, a_rate, d_skip, gain):
    rows, width = x_in.shape
    heads = dt_bias.shape[0]
    hdim = width // heads
    per = heads // GROUPS
    unit = per * hdim
    count = conv_x.shape[0]
    axis = "ctx"
    n = lax.axis_size(axis)
    plane = plane_size(n, GROUPS)
    planes = n // plane
    chunks = GROUPS // plane
    bits = plane.bit_length() - 1
    index = lax.axis_index(axis)
    j = index % plane
    z = index // plane
    scale = 2.0**-max(0, 1 + int(n * rows * DT_TOP * PEAK * PEAK / 65504.0).bit_length())

    def swap(v, bit):
        return lax.ppermute(v, axis, [(i, i ^ (1 << bit)) for i in range(n)])

    def send(v, move):
        return move((v * scale).astype(WIRE)).astype(F32) * (1.0 / scale)

    ends = jnp.concatenate([x_in[rows - (count - 1) :], bc_in[rows - (count - 1) :]], axis=1)
    rim = lax.ppermute(ends, axis, [(i, i + 1) for i in range(n - 1)])
    rim_x = rim[:, :width]
    rim_bc = rim[:, width:]

    small = [
        jax.ShapeDtypeStruct((GROUPS, rows, per), F32),
        jax.ShapeDtypeStruct((GROUPS, rows, per), F32),
        jax.ShapeDtypeStruct((GROUPS, per, rows), F32),
        jax.ShapeDtypeStruct((GROUPS, rows + 8, per), F32),
        jax.ShapeDtypeStruct((1, heads), F32),
    ]
    tail, cum, row, ecum, total = pl.pallas_call(steps_kernel, out_shape=small)(
        dt_in, dt_bias[None], a_rate[None], d_skip[None]
    )
    logs = total
    for bit in range(bits):
        logs = jnp.concatenate([logs, swap(logs, bit)], axis=0)

    head_map = (jnp.arange(unit)[None, :] // hdim == jnp.arange(per)[:, None]).astype(BF16)
    head_map = jnp.concatenate([head_map] * 3, axis=0)

    def flip(p):
        return int(format(p, f"0{bits}b")[::-1], 2) if bits else 0

    def orders(chunk, positions):
        return jnp.stack([(j ^ flip(p)) * chunks + chunk for p in positions]).astype(jnp.int32)

    def group_rows(log, order):
        values = jnp.exp(log).reshape(GROUPS, per)
        values = jnp.concatenate([lax.dynamic_slice_in_dim(values, order[k], 1, 0) for k in range(order.shape[0])], axis=0)
        return jnp.broadcast_to(values[:, :, None], (*values.shape, hdim)).reshape(values.shape[0], 1, unit)

    def at_group(shape, base=0):
        return pl.BlockSpec(shape, lambda s, o: (0, o[s] + base))

    def at_lead(shape):
        return pl.BlockSpec(shape, lambda s, o: (o[s], 0, 0))

    def in_set(shape):
        return pl.BlockSpec(shape, lambda s, o: (s, 0, 0))

    whole_map = pl.BlockSpec(head_map.shape, lambda s, o: (0, 0))

    def states(order):
        size = order.shape[0]
        return call(
            state_kernel,
            order,
            [jax.ShapeDtypeStruct((size, STATE, unit), F32), jax.ShapeDtypeStruct((size, rows, unit), F32)],
            [
                at_group((rows, unit)),
                at_group((count - 1, unit)),
                at_group((count, unit)),
                at_group((rows, STATE)),
                at_group((count - 1, STATE)),
                at_group((count, STATE)),
                at_lead((1, rows, per)),
                whole_map,
            ],
            [in_set((1, STATE, unit)), in_set((1, rows, unit))],
            (x_in, rim_x, conv_x, bc_in, rim_bc, conv_bc, tail, head_map),
        )

    def local(order, xc):
        size = order.shape[0]
        return call(
            local_kernel,
            order,
            [jax.ShapeDtypeStruct((size, rows, unit), F32)] * 2 + [jax.ShapeDtypeStruct((size, rows, STATE), F32)],
            [
                at_group((rows, STATE)),
                at_group((count - 1, STATE)),
                at_group((count, STATE)),
                at_group((rows, STATE), GROUPS),
                at_group((count - 1, STATE), GROUPS),
                at_group((count, STATE), GROUPS),
                in_set((1, rows, unit)),
                at_lead((1, rows, per)),
                at_lead((1, per, rows)),
                at_lead((1, rows + 8, per)),
                whole_map,
                at_group((rows, unit)),
            ],
            [in_set((1, rows, unit)), in_set((1, rows, unit)), in_set((1, rows, STATE))],
            (bc_in, rim_bc, conv_bc, bc_in, rim_bc, conv_bc, xc, cum, row, ecum, head_map, z_in),
        )

    def finish(order, before, c, m1, m2, out):
        spec = at_group((rows, unit))
        return call(
            finish_kernel,
            order,
            jax.ShapeDtypeStruct((rows, width), BF16),
            [
                in_set((1, STATE, unit)),
                in_set((1, rows, STATE)),
                in_set((1, rows, unit)),
                in_set((1, rows, unit)),
                at_group((1, unit)),
                pl.BlockSpec(memory_space=pl.ANY),
            ],
            spec,
            (before, c, m1, m2, gain[None], out),
            input_output_aliases={6: 0},
        )

    half = plane // 2
    sets = []
    for chunk in range(chunks):
        far = orders(chunk, range(half, plane))
        near = orders(chunk, range(half))
        sets.append((far, near))

    def upper(bit):
        return (j >> bit) & 1 == 1

    own_log, other_log = [], []
    for bit in range(bits):
        own_log.append(jnp.sum(logs[: 1 << bit], axis=0))
        other_log.append(jnp.sum(logs[1 << bit : 2 << bit], axis=0))

    levels, tops, top_rows, locals_ = [], [], [], []
    for chunk in range(chunks):
        far, near = sets[chunk]
        s_far, xc_far = states(far)
        s_near, xc_near = states(near)
        locals_.append(((far, xc_far), (near, xc_near)))
        keep, give = s_near, s_far
        stack = []
        for bit in range(bits):
            got = send(give, functools.partial(swap, bit=bit))
            order = orders(chunk, range(keep.shape[0]))
            lower_row = group_rows(jnp.where(upper(bit), other_log[bit], own_log[bit]), order)
            upper_row = group_rows(jnp.where(upper(bit), own_log[bit], other_log[bit]), order)
            lower_state = jnp.where(upper(bit), got, keep)
            upper_state = jnp.where(upper(bit), keep, got)
            both = lower_state * upper_row + upper_state
            stack.append((lower_row, lower_state))
            cut = both.shape[0] // 2
            keep, give = (both[:cut], both[cut:]) if cut else (both, None)
        levels.append(stack)
        tops.append(keep)
        top_rows.append(group_rows(jnp.sum(logs, axis=0), orders(chunk, [0])))

    pairs = [(i, i + plane) for i in range(n - plane)]
    entering = [jnp.zeros_like(tops[0])]
    for step in range(chunks + planes - 2 if planes > 1 else 0):
        which = jnp.clip(step - z, 0, chunks - 1)
        top, top_row = tops[0], top_rows[0]
        for chunk in range(1, chunks):
            top = jnp.where(which == chunk, tops[chunk], top)
            top_row = jnp.where(which == chunk, top_rows[chunk], top_row)
        entering.append(send(top_row * entering[-1] + top, lambda v: lax.ppermute(v, axis, pairs)))

    mixes = []
    for chunk in range(chunks):
        mixes.append([local(*one) for one in locals_[chunk]])

    out = pl.empty((rows, width), BF16) if False else jnp.zeros((rows, width), BF16)
    for chunk in range(chunks):
        state = entering[chunk]
        for at in range(1, planes):
            if chunk + at < len(entering):
                state = jnp.where(z == at, entering[chunk + at], state)
        state = jnp.where(z == 0, 0.0, state)
        other = None
        for bit in reversed(range(bits)):
            lower_row, lower_state = levels[chunk][bit]
            later = lower_row * state + lower_state
            other = send(jnp.where(upper(bit), state, later), functools.partial(swap, bit=bit))
            state = jnp.where(upper(bit), later, state)
            if bit:
                state = jnp.concatenate([state, other], axis=0)
        far, near = sets[chunk]
        m_far, m_near = mixes[chunk]
        out = finish(near, state, m_near[2], m_near[0], m_near[1], out)
        out = finish(far, other, m_far[2], m_far[0], m_far[1], out)
    return out


def solution(mesh):
    split_rows = P(("groups", "ctx"), None)
    return jax.shard_map(
        shards,
        mesh=mesh,
        in_specs=(split_rows,) * 4 + (P(),) * 6,
        out_specs=split_rows,
        check_vma=False,
    )
```

time: 355 us -> 152 us (0.43)
  waiting for transfers between devices: 183 us -> 29.5 us
  Pallas kernels: 0 us -> 56.3 us
  local copies, waits for them, and re-layouts: 55.6 us -> 7.4 us
  other arithmetic: 58.5 us -> 27.9 us
  matrix products: 30.1 us -> 0 us
  starting transfers between devices: 22.3 us -> 29 us
    all_to_all x3 -> x0, waiting for transfers between devices: 183 us -> none  [the longest x1 91.7 us: shards(): lax.all_to_all(flat, 'ctx', split_axis=1, concat_axis=0, tiled=True)]
    pallas_call x0 -> x13, Pallas kernels: none -> 56.3 us  [the longest x12 53.9 us: call(): pl.pallas_call(body, out_shape=out_shape, grid_spec=grid_spec, **more)]
    dot_general x4 -> x0, matrix products: 30.1 us -> none  [the longest x1 18.1 us: block_terms(): y_diag = jnp.einsum('gkts,sgkp->tgkp', weights, xg, precision=HIGH)]
    ppermute x1 -> x15, waiting for transfers between devices: 0.39 us -> 29.5 us  [the longest x4 17.7 us: shards(): lax.ppermute(v, axis, pairs)]
    ppermute x1 -> x15, starting transfers between devices: 3.54 us -> 29 us  [the longest x4 13 us: shards(): lax.ppermute(v, axis, pairs)]
    unnamed x40 -> x12, local copies, waits for them, and re-layouts: 21 us -> 0.81 us
    all_to_all x3 -> x0, starting transfers between devices: 18.7 us -> none  [the longest x1 6.94 us: shards(): lax.all_to_all(flat, 'ctx', split_axis=1, concat_axis=0, tiled=True)]
    add x9 -> x2, other arithmetic: 16.5 us -> 2.56 us  [shards(): both = lower_state * upper_row + upper_state]
  transfers between devices with their start and end apart: 4 -> 15, of which waited for: 3 -> 8; matrix products, arithmetic and copies ran while one was open for 13% -> 15% of each run, Pallas kernels for 0% -> 30%
where the time goes in v1:
time: 152 us; the launch traced here: 150 us
  Pallas kernels  56.3 us (37%)
  waiting for transfers between devices  29.5 us (19%)
  starting transfers between devices  29 us (19%)
  other arithmetic  27.9 us (18%)
  local copies, waits for them, and re-layouts  7.4 us (5%)
    pallas_call x12, Pallas kernels, call(): pl.pallas_call(body, out_shape=out_shape, grid_spec=grid_spec, **more)  53.9 us
    ppermute x4, waiting for transfers between devices, shards(): lax.ppermute(v, axis, pairs)  17.7 us
    ppermute x4, starting transfers between devices, shards(): lax.ppermute(v, axis, pairs)  13 us
    ppermute x10, starting transfers between devices, swap(): return lax.ppermute(v, axis, [(i, i ^ 1 << bit) for i in range(n)])  13 us
    ppermute x10, waiting for transfers between devices, swap(): return lax.ppermute(v, axis, [(i, i ^ 1 << bit) for i in range(n)])  11.8 us
    convert_element_type x7, other arithmetic, send(): return move((v * scale).astype(WIRE)).astype(F32) * (1.0 / scale)  11 us
    select_n x4, other arithmetic, shards(): state = jnp.where(upper(bit), later, state)  7.93 us
    ppermute x1, starting transfers between devices, shards(): rim = lax.ppermute(ends, axis, [(i, i + 1) for i in range(n - 1)])  3.06 us
  transfers between devices with their start and end apart: 15, of which 8 were waited for; matrix products, arithmetic and copies ran while one was open for 15% of the time, Pallas kernels for 30%

profile of v1, /device:TPU:11, one launch (start us, length us, event | category | flops | bytes accessed | tf_op | source)
XLA Modules:
  0.0 150.4 jit_solution(909162288762743995)
XLA Ops:
  4.9 3.1 %collective-permute-start.2 = (bf16[3,10240]{1,0:T(4,128)(2,1)S(1)}, bf16[3,10240]{1,0:T(4,128)(2,1)S(1)}, u32[]{:S(2)}, u32[]{:S(2)}) collective-permute-start(bf16[3,10240]{1,0:T(4,128)(2,1)S(1)} %pad_maximum_fusion.2), channel_id=1, source_target_pairs={{0,1},{1,2},{2,3},{3,4},{4,5},{5,6},{6,7},{7,8},{8,9},{9,10},{10,1... | collective-permute-start | bytes 184328 | tf_op jit(solution)/shard_map/ppermute | solution.py:171
  16.1 4.5 %shard_map.103 = (f32[2,128,1024]{2,1,0:T(8,128)}, f32[2,128,1024]{2,1,0:T(8,128)}) custom-call(s32[2]{0:T(128)} %get-tuple-element.89.order_ref, bf16[128,8192]{1,0:T(8,128)(2,1)} %x_ref.7, bf16[3,8192]{1,0:T(4,128)(2,1)} %slice.32.xh_ref, f32[4,8192]{1,0:T(4,128)} %tx_ref.7, bf16[128,2048]{1,0:T(8,128)(2,1)} %c_ref.7, ...), custom_call_target="tpu_custom_call" | custom-call | tf_op jit(solution)/shard_map/pallas_call | solution.py:143
  22.4 4.6 %shard_map.104 = (f32[2,128,1024]{2,1,0:T(8,128)}, f32[2,128,1024]{2,1,0:T(8,128)}) custom-call(s32[2]{0:T(128)} %pad_add_fusion.3.order_ref, bf16[128,8192]{1,0:T(8,128)(2,1)} %x_ref.7, bf16[3,8192]{1,0:T(4,128)(2,1)} %slice.32.xh_ref, f32[4,8192]{1,0:T(4,128)} %tx_ref.7, bf16[128,2048]{1,0:T(8,128)(2,1)} %c_ref.7, bf16[3,2048]{1,0:T(4,128)(2,1)} %slice.33.bh_ref.ch_ref, ...), custom_call_target="tpu_custom_call" | custom-call | tf_op jit(solution)/shard_map/pallas_call | solution.py:143
  27.0 4.5 %shard_map.101 = (f32[2,128,1024]{2,1,0:T(8,128)}, f32[2,128,1024]{2,1,0:T(8,128)}) custom-call(s32[2]{0:T(128)} %pad_add_fusion.order_ref, bf16[128,8192]{1,0:T(8,128)(2,1)} %x_ref.7, bf16[3,8192]{1,0:T(4,128)(2,1)} %slice.32.xh_ref, f32[4,8192]{1,0:T(4,128)} %tx_ref.7, bf16[128,2048]{1,0:T(8,128)(2,1)} %c_ref.7, bf16[3,2048]{1,0:T(4,128)(2,1)} %slice.33.bh_ref.ch_ref, ...), custom_call_target="tpu_custom_call" | custom-call | tf_op jit(solution)/shard_map/pallas_call | solution.py:143
  33.8 4.7 %shard_map.102 = (f32[2,128,1024]{2,1,0:T(8,128)}, f32[2,128,1024]{2,1,0:T(8,128)}) custom-call(s32[2]{0:T(128)} %get-tuple-element.88.order_ref, bf16[128,8192]{1,0:T(8,128)(2,1)} %x_ref.7, bf16[3,8192]{1,0:T(4,128)(2,1)} %slice.32.xh_ref, f32[4,8192]{1,0:T(4,128)} %tx_ref.7, bf16[128,2048]{1,0:T(8,128)(2,1)} %c_ref.7, ...), custom_call_target="tpu_custom_call" | custom-call | tf_op jit(solution)/shard_map/pallas_call | solution.py:143
  45.3 4.0 %collective-permute-done.6 = f16[1,128,1024]{2,1,0:T(8,128)(2,1)} collective-permute-done((f16[1,128,1024]{2,1,0:T(8,128)(2,1)}, f16[1,128,1024]{2,1,0:T(8,128)(2,1)}, u32[]{:S(2)}, u32[]{:S(2)}) %collective-permute-start.6) | collective-permute-done | bytes 262176 | tf_op jit(solution)/shard_map/ppermute | solution.py:165
  49.3 5.5 %collective-permute-done.4 = f16[1,128,1024]{2,1,0:T(8,128)(2,1)S(1)} collective-permute-done((f16[1,128,1024]{2,1,0:T(8,128)(2,1)}, f16[1,128,1024]{2,1,0:T(8,128)(2,1)S(1)}, u32[]{:S(2)}, u32[]{:S(2)}) %collective-permute-start.4) | collective-permute-done | bytes 262176 | tf_op jit(solution)/shard_map/ppermute | solution.py:165
  56.7 3.2 %collective-permute-start.7 = (f16[1,128,1024]{2,1,0:T(8,128)(2,1)}, f16[1,128,1024]{2,1,0:T(8,128)(2,1)}, u32[]{:S(2)}, u32[]{:S(2)}) collective-permute-start(f16[1,128,1024]{2,1,0:T(8,128)(2,1)} %multiply_convert_fusion.6), channel_id=1, source_target_pairs={{0,4},{1,5},{2,6},{3,7},{4,8},{5,9},{6,10},{7,11},{8,12},{9,13},{1... | collective-permute-start | bytes 786440 | tf_op jit(solution)/shard_map/ppermute | solution.py:323
  60.1 5.6 %collective-permute-done.7 = f16[1,128,1024]{2,1,0:T(8,128)(2,1)} collective-permute-done((f16[1,128,1024]{2,1,0:T(8,128)(2,1)}, f16[1,128,1024]{2,1,0:T(8,128)(2,1)}, u32[]{:S(2)}, u32[]{:S(2)}) %collective-permute-start.7) | collective-permute-done | bytes 262176 | tf_op jit(solution)/shard_map/ppermute | solution.py:323
  67.7 3.2 %collective-permute-start.8 = (f16[1,128,1024]{2,1,0:T(8,128)(2,1)}, f16[1,128,1024]{2,1,0:T(8,128)(2,1)}, u32[]{:S(2)}, u32[]{:S(2)}) collective-permute-start(f16[1,128,1024]{2,1,0:T(8,128)(2,1)} %fusion.14), channel_id=1, source_target_pairs={{0,4},{1,5},{2,6},{3,7},{4,8},{5,9},{6,10},{7,11},{8,12},{9,13},{1... | collective-permute-start | bytes 786440 | tf_op jit(solution)/shard_map/ppermute | solution.py:323
  71.0 4.8 %collective-permute-done.8 = f16[1,128,1024]{2,1,0:T(8,128)(2,1)} collective-permute-done((f16[1,128,1024]{2,1,0:T(8,128)(2,1)}, f16[1,128,1024]{2,1,0:T(8,128)(2,1)}, u32[]{:S(2)}, u32[]{:S(2)}) %collective-permute-start.8) | collective-permute-done | bytes 262176 | tf_op jit(solution)/shard_map/ppermute | solution.py:323
  77.9 3.2 %collective-permute-start.9 = (f16[1,128,1024]{2,1,0:T(8,128)(2,1)}, f16[1,128,1024]{2,1,0:T(8,128)(2,1)}, u32[]{:S(2)}, u32[]{:S(2)}) collective-permute-start(f16[1,128,1024]{2,1,0:T(8,128)(2,1)} %fusion.17), channel_id=1, source_target_pairs={{0,4},{1,5},{2,6},{3,7},{4,8},{5,9},{6,10},{7,11},{8,12},{9,13},{1... | collective-permute-start | bytes 786440 | tf_op jit(solution)/shard_map/ppermute | solution.py:323
  81.3 4.0 %collective-permute-done.9 = f16[1,128,1024]{2,1,0:T(8,128)(2,1)} collective-permute-done((f16[1,128,1024]{2,1,0:T(8,128)(2,1)}, f16[1,128,1024]{2,1,0:T(8,128)(2,1)}, u32[]{:S(2)}, u32[]{:S(2)}) %collective-permute-start.9) | collective-permute-done | bytes 262176 | tf_op jit(solution)/shard_map/ppermute | solution.py:323
  88.0 3.5 %collective-permute-start.10 = (f16[1,128,1024]{2,1,0:T(8,128)(2,1)}, f16[1,128,1024]{2,1,0:T(8,128)(2,1)}, u32[]{:S(2)}, u32[]{:S(2)}) collective-permute-start(f16[1,128,1024]{2,1,0:T(8,128)(2,1)} %get-tuple-element.69), channel_id=1, source_target_pairs={{0,4},{1,5},{2,6},{3,7},{4,8},{5,9},{6,10},{7,11},{8,12},{9,13},{1... | collective-permute-start | bytes 786440 | tf_op jit(solution)/shard_map/ppermute | solution.py:323
  92.2 3.3 %collective-permute-done.10 = f16[1,128,1024]{2,1,0:T(8,128)(2,1)} collective-permute-done((f16[1,128,1024]{2,1,0:T(8,128)(2,1)}, f16[1,128,1024]{2,1,0:T(8,128)(2,1)}, u32[]{:S(2)}, u32[]{:S(2)}) %collective-permute-start.10) | collective-permute-done | bytes 262176 | tf_op jit(solution)/shard_map/ppermute | solution.py:323
  99.2 7.5 %collective-permute-start.14 = (f16[2,128,1024]{2,1,0:T(8,128)(2,1)S(1)}, f16[2,128,1024]{2,1,0:T(8,128)(2,1)S(1)}, u32[]{:S(2)}, u32[]{:S(2)}) collective-permute-start(f16[2,128,1024]{2,1,0:T(8,128)(2,1)S(1)} %get-tuple-element.62), channel_id=1, source_target_pairs={{0,1},{1,0},{2,3},{3,2},{4,5},{5,4},{6,7},{7,6},{8,9},{9,8},{10,11... | collective-permute-start | bytes 1572872 | tf_op jit(solution)/shard_map/ppermute | solution.py:165
  111.1 5.2 %shard_map.108 = (f32[2,128,1024]{2,1,0:T(8,128)}, f32[2,128,1024]{2,1,0:T(8,128)}, f32[2,128,128]{2,1,0:T(8,128)}) custom-call(s32[2]{0:T(128)} %pad_add_fusion.3.order_ref, bf16[128,2048]{1,0:T(8,128)(2,1)} %c_ref.7, bf16[3,2048]{1,0:T(4,128)(2,1)} %slice.33.bh_ref.ch_ref, f32[4,2048]{1,0:T(4,128)} %tc_ref.7, bf16[128,2048]{1,0:T(8,128)(2,1)} %c_ref.7, ...), custom_call_target="tpu_custom_call" | custom-call | tf_op jit(solution)/shard_map/pallas_call | solution.py:143
  116.3 5.2 %shard_map.107 = (f32[2,128,1024]{2,1,0:T(8,128)}, f32[2,128,1024]{2,1,0:T(8,128)}, f32[2,128,128]{2,1,0:T(8,128)}) custom-call(s32[2]{0:T(128)} %get-tuple-element.89.order_ref, bf16[128,2048]{1,0:T(8,128)(2,1)} %c_ref.7, bf16[3,2048]{1,0:T(4,128)(2,1)} %slice.33.bh_ref.ch_ref, f32[4,2048]{1,0:T(4,128)} %tc_ref.7, bf16[128,2048]{1,0:T(8,128)(2,1)} %c_ref.7, ...), custom_call_target="tpu_custom_call" | custom-call | tf_op jit(solution)/shard_map/pallas_call | solution.py:143
  121.4 5.2 %shard_map.106 = (f32[2,128,1024]{2,1,0:T(8,128)}, f32[2,128,1024]{2,1,0:T(8,128)}, f32[2,128,128]{2,1,0:T(8,128)}) custom-call(s32[2]{0:T(128)} %get-tuple-element.88.order_ref, bf16[128,2048]{1,0:T(8,128)(2,1)} %c_ref.7, bf16[3,2048]{1,0:T(4,128)(2,1)} %slice.33.bh_ref.ch_ref, f32[4,2048]{1,0:T(4,128)} %tc_ref.7, bf16[128,2048]{1,0:T(8,128)(2,1)} %c_ref.7, ...), custom_call_target="tpu_custom_call" | custom-call | tf_op jit(solution)/shard_map/pallas_call | solution.py:143
  126.6 5.2 %shard_map.105 = (f32[2,128,1024]{2,1,0:T(8,128)}, f32[2,128,1024]{2,1,0:T(8,128)}, f32[2,128,128]{2,1,0:T(8,128)}) custom-call(s32[2]{0:T(128)} %pad_add_fusion.order_ref, bf16[128,2048]{1,0:T(8,128)(2,1)} %c_ref.7, bf16[3,2048]{1,0:T(4,128)(2,1)} %slice.33.bh_ref.ch_ref, f32[4,2048]{1,0:T(4,128)} %tc_ref.7, bf16[128,2048]{1,0:T(8,128)(2,1)} %c_ref.7, ...), custom_call_target="tpu_custom_call" | custom-call | tf_op jit(solution)/shard_map/pallas_call | solution.py:143
  133.3 3.7 %shard_map.109.held_ref = bf16[128,8192]{1,0:T(8,128)(2,1)} custom-call(s32[2]{0:T(128)} %pad_add_fusion.3.order_ref, f32[2,128,1024]{2,1,0:T(8,128)} %get-tuple-element.61.p_ref, f32[2,128,128]{2,1,0:T(8,128)} %get-tuple-element.52.c_ref, f32[2,128,1024]{2,1,0:T(8,128)} %get-tuple-element.53.m1_ref, ...), custom_call_target="tpu_custom_call", output_to_operand_aliasing={{}: (6, {})} | custom-call | tf_op jit(solution)/shard_map/pallas_call | solution.py:143
  138.2 3.7 %shard_map.110.held_ref = bf16[128,8192]{1,0:T(8,128)(2,1)} custom-call(s32[2]{0:T(128)} %get-tuple-element.89.order_ref, f32[2,128,1024]{2,1,0:T(8,128)} %convert_multiply_fusion.p_ref, f32[2,128,128]{2,1,0:T(8,128)} %get-tuple-element.48.c_ref, f32[2,128,1024]{2,1,0:T(8,128)} %get-tuple-element.49.m1_ref, ...), custom_call_target="tpu_custom_call", output_to_operand_aliasing={{}: (6, {})} | custom-call | tf_op jit(solution)/shard_map/pallas_call | solution.py:143
  141.9 3.7 %shard_map.111.held_ref = bf16[128,8192]{1,0:T(8,128)(2,1)} custom-call(s32[2]{0:T(128)} %get-tuple-element.88.order_ref, f32[2,128,1024]{2,1,0:T(8,128)} %get-tuple-element.63.p_ref, f32[2,128,128]{2,1,0:T(8,128)} %get-tuple-element.44.c_ref, f32[2,128,1024]{2,1,0:T(8,128)} %get-tuple-element.45.m1_ref, ...), custom_call_target="tpu_custom_call", output_to_operand_aliasing={{}: (6, {})} | custom-call | tf_op jit(solution)/shard_map/pallas_call | solution.py:143
  146.7 3.7 %shard_map.112 = bf16[128,8192]{1,0:T(8,128)(2,1)} custom-call(s32[2]{0:T(128)} %pad_add_fusion.order_ref, f32[2,128,1024]{2,1,0:T(8,128)} %convert_multiply_fusion.1.p_ref, f32[2,128,128]{2,1,0:T(8,128)} %get-tuple-element.40.c_ref, f32[2,128,1024]{2,1,0:T(8,128)} %get-tuple-element.41.m1_ref, ...), custom_call_target="tpu_custom_call", output_to_operand_aliasing={{}: (6, {})} | custom-call | tf_op jit(solution)/shard_map/pallas_call | solution.py:143
  (100 shorter events, 45.5 us)
Async XLA Ops:
  2.5 8.1 %collective-permute-start = (f32[1,128]{1,0:T(1,128)}, f32[1,128]{1,0:T(1,128)S(1)}, u32[]{:S(2)}, u32[]{:S(2)}) collective-permute-start(f32[1,128]{1,0:T(1,128)} %get-tuple-element.30), channel_id=1, source_target_pairs={{0,1},{1,0},{2,3},{3,2},{4,5},{5,4},{6,7},{7,6},{8,9},{9,8},{10,11... | collective-permute-start | bytes 1544 | tf_op jit(solution)/shard_map/ppermute | solution.py:165
  4.9 9.9 %collective-permute-start.2 = (bf16[3,10240]{1,0:T(4,128)(2,1)S(1)}, bf16[3,10240]{1,0:T(4,128)(2,1)S(1)}, u32[]{:S(2)}, u32[]{:S(2)}) collective-permute-start(bf16[3,10240]{1,0:T(4,128)(2,1)S(1)} %pad_maximum_fusion.2), channel_id=1, source_target_pairs={{0,1},{1,2},{2,3},{3,4},{4,5},{5,6},{6,7},{7,8},{8,9},{9,10},{10,1... | collective-permute-start | bytes 184328 | tf_op jit(solution)/shard_map/ppermute | solution.py:171
  12.2 2.5 %collective-permute-start.1 = (f32[2,128]{1,0:T(2,128)S(1)}, f32[2,128]{1,0:T(2,128)S(1)}, u32[]{:S(2)}, u32[]{:S(2)}) collective-permute-start(f32[2,128]{1,0:T(2,128)S(1)} %pad_maximum_fusion.3), channel_id=1, source_target_pairs={{0,2},{1,3},{2,0},{3,1},{4,6},{5,7},{6,4},{7,5},{8,10},{9,11},{10,... | collective-permute-start | bytes 3080 | tf_op jit(solution)/shard_map/ppermute | solution.py:165
  22.0 16.5 %collective-permute-start.5 = (f16[2,128,1024]{2,1,0:T(8,128)(2,1)S(1)}, f16[2,128,1024]{2,1,0:T(8,128)(2,1)S(1)}, u32[]{:S(2)}, u32[]{:S(2)}) collective-permute-start(f16[2,128,1024]{2,1,0:T(8,128)(2,1)S(1)} %multiply_convert_fusion.2), channel_id=1, source_target_pairs={{0,1},{1,0},{2,3},{3,2},{4,5},{5,4},{6,7},{7,6},{8,9},{9,8},{10,11... | collective-permute-start | bytes 1572872 | tf_op jit(solution)/shard_map/ppermute | solution.py:165
  33.7 5.6 %copy-start.1 = (f32[2,128,1024]{2,1,0:T(8,128)S(1)}, f32[2,128,1024]{2,1,0:T(8,128)}, u32[]{:S(2)}) copy-start(f32[2,128,1024]{2,1,0:T(8,128)} %get-tuple-element.35) | copy-start | bytes 3145732
  33.7 7.9 %collective-permute-start.3 = (f16[2,128,1024]{2,1,0:T(8,128)(2,1)}, f16[2,128,1024]{2,1,0:T(8,128)(2,1)}, u32[]{:S(2)}, u32[]{:S(2)}) collective-permute-start(f16[2,128,1024]{2,1,0:T(8,128)(2,1)} %multiply_convert_fusion.3), channel_id=1, source_target_pairs={{0,1},{1,0},{2,3},{3,2},{4,5},{5,4},{6,7},{7,6},{8,9},{9,8},{10,11... | collective-permute-start | bytes 1572872 | tf_op jit(solution)/shard_map/ppermute | solution.py:165
  38.5 3.1 %copy-start = (f32[2,128,1024]{2,1,0:T(8,128)S(1)}, f32[2,128,1024]{2,1,0:T(8,128)}, u32[]{:S(2)}) copy-start(f32[2,128,1024]{2,1,0:T(8,128)} %get-tuple-element.33) | copy-start | bytes 3145732
  38.5 0.8 copy-start.3
  41.3 7.9 %collective-permute-start.6 = (f16[1,128,1024]{2,1,0:T(8,128)(2,1)}, f16[1,128,1024]{2,1,0:T(8,128)(2,1)}, u32[]{:S(2)}, u32[]{:S(2)}) collective-permute-start(f16[1,128,1024]{2,1,0:T(8,128)(2,1)} %fusion.21), channel_id=1, source_target_pairs={{0,2},{1,3},{2,0},{3,1},{4,6},{5,7},{6,4},{7,5},{8,10},{9,11},{10,... | collective-permute-start | bytes 786440 | tf_op jit(solution)/shard_map/ppermute | solution.py:165
  43.6 11.1 %collective-permute-start.4 = (f16[1,128,1024]{2,1,0:T(8,128)(2,1)}, f16[1,128,1024]{2,1,0:T(8,128)(2,1)S(1)}, u32[]{:S(2)}, u32[]{:S(2)}) collective-permute-start(f16[1,128,1024]{2,1,0:T(8,128)(2,1)} %fusion.22), channel_id=1, source_target_pairs={{0,2},{1,3},{2,0},{3,1},{4,6},{5,7},{6,4},{7,5},{8,10},{9,11},{10,... | collective-permute-start | bytes 786440 | tf_op jit(solution)/shard_map/ppermute | solution.py:165
  56.7 9.0 %collective-permute-start.7 = (f16[1,128,1024]{2,1,0:T(8,128)(2,1)}, f16[1,128,1024]{2,1,0:T(8,128)(2,1)}, u32[]{:S(2)}, u32[]{:S(2)}) collective-permute-start(f16[1,128,1024]{2,1,0:T(8,128)(2,1)} %multiply_convert_fusion.6), channel_id=1, source_target_pairs={{0,4},{1,5},{2,6},{3,7},{4,8},{5,9},{6,10},{7,11},{8,12},{9,13},{1... | collective-permute-start | bytes 786440 | tf_op jit(solution)/shard_map/ppermute | solution.py:323
  67.7 8.1 %collective-permute-start.8 = (f16[1,128,1024]{2,1,0:T(8,128)(2,1)}, f16[1,128,1024]{2,1,0:T(8,128)(2,1)}, u32[]{:S(2)}, u32[]{:S(2)}) collective-permute-start(f16[1,128,1024]{2,1,0:T(8,128)(2,1)} %fusion.14), channel_id=1, source_target_pairs={{0,4},{1,5},{2,6},{3,7},{4,8},{5,9},{6,10},{7,11},{8,12},{9,13},{1... | collective-permute-start | bytes 786440 | tf_op jit(solution)/shard_map/ppermute | solution.py:323
  77.9 7.4 %collective-permute-start.9 = (f16[1,128,1024]{2,1,0:T(8,128)(2,1)}, f16[1,128,1024]{2,1,0:T(8,128)(2,1)}, u32[]{:S(2)}, u32[]{:S(2)}) collective-permute-start(f16[1,128,1024]{2,1,0:T(8,128)(2,1)} %fusion.17), channel_id=1, source_target_pairs={{0,4},{1,5},{2,6},{3,7},{4,8},{5,9},{6,10},{7,11},{8,12},{9,13},{1... | collective-permute-start | bytes 786440 | tf_op jit(solution)/shard_map/ppermute | solution.py:323
  88.0 9.9 %copy-start.2 = (f32[2,128,1024]{2,1,0:T(8,128)S(1)}, f32[2,128,1024]{2,1,0:T(8,128)}, u32[]{:S(2)}) copy-start(f32[2,128,1024]{2,1,0:T(8,128)} %get-tuple-element.35) | copy-start | bytes 3145732
  88.0 7.6 %collective-permute-start.10 = (f16[1,128,1024]{2,1,0:T(8,128)(2,1)}, f16[1,128,1024]{2,1,0:T(8,128)(2,1)}, u32[]{:S(2)}, u32[]{:S(2)}) collective-permute-start(f16[1,128,1024]{2,1,0:T(8,128)(2,1)} %get-tuple-element.69), channel_id=1, source_target_pairs={{0,4},{1,5},{2,6},{3,7},{4,8},{5,9},{6,10},{7,11},{8,12},{9,13},{1... | collective-permute-start | bytes 786440 | tf_op jit(solution)/shard_map/ppermute | solution.py:323
  91.9 5.9 %copy-start.4 = (f16[2,128,1024]{2,1,0:T(8,128)(2,1)S(1)}, f16[2,128,1024]{2,1,0:T(8,128)(2,1)}, u32[]{:S(2)}) copy-start(f16[2,128,1024]{2,1,0:T(8,128)(2,1)} %copy-done.3) | copy-start | bytes 1572868
  91.9 5.9 %copy-start.5 = (f32[1,128,1024]{2,1,0:T(8,128)S(1)}, f32[1,128,1024]{2,1,0:T(8,128)}, u32[]{:S(2)}) copy-start(f32[1,128,1024]{2,1,0:T(8,128)} %get-tuple-element.67) | copy-start | bytes 1572868
  91.9 5.8 %collective-permute-start.13 = (f16[1,128,1024]{2,1,0:T(8,128)(2,1)}, f16[1,128,1024]{2,1,0:T(8,128)(2,1)S(1)}, u32[]{:S(2)}, u32[]{:S(2)}) collective-permute-start(f16[1,128,1024]{2,1,0:T(8,128)(2,1)} %get-tuple-element.68), channel_id=1, source_target_pairs={{0,2},{1,3},{2,0},{3,1},{4,6},{5,7},{6,4},{7,5},{8,10},{9,11},{10,... | collective-permute-start | bytes 786440 | tf_op jit(solution)/shard_map/ppermute | solution.py:165
  97.1 9.6 %collective-permute-start.11 = (f16[1,128,1024]{2,1,0:T(8,128)(2,1)S(1)}, f16[1,128,1024]{2,1,0:T(8,128)(2,1)S(1)}, u32[]{:S(2)}, u32[]{:S(2)}) collective-permute-start(f16[1,128,1024]{2,1,0:T(8,128)(2,1)S(1)} %get-tuple-element.66), channel_id=1, source_target_pairs={{0,2},{1,3},{2,0},{3,1},{4,6},{5,7},{6,4},{7,5},{8,10},{9,11},{10,... | collective-permute-start | bytes 786440 | tf_op jit(solution)/shard_map/ppermute | solution.py:165
  99.2 37.8 %collective-permute-start.14 = (f16[2,128,1024]{2,1,0:T(8,128)(2,1)S(1)}, f16[2,128,1024]{2,1,0:T(8,128)(2,1)S(1)}, u32[]{:S(2)}, u32[]{:S(2)}) collective-permute-start(f16[2,128,1024]{2,1,0:T(8,128)(2,1)S(1)} %get-tuple-element.62), channel_id=1, source_target_pairs={{0,1},{1,0},{2,3},{3,2},{4,5},{5,4},{6,7},{7,6},{8,9},{9,8},{10,11... | collective-permute-start | bytes 1572872 | tf_op jit(solution)/shard_map/ppermute | solution.py:165
  109.2 36.4 %collective-permute-start.12 = (f16[2,128,1024]{2,1,0:T(8,128)(2,1)S(1)}, f16[2,128,1024]{2,1,0:T(8,128)(2,1)S(1)}, u32[]{:S(2)}, u32[]{:S(2)}) collective-permute-start(f16[2,128,1024]{2,1,0:T(8,128)(2,1)S(1)} %get-tuple-element.64), channel_id=1, source_target_pairs={{0,1},{1,0},{2,3},{3,2},{4,5},{5,4},{6,7},{7,6},{8,9},{9,8},{10,11... | collective-permute-start | bytes 1572872 | tf_op jit(solution)/shard_map/ppermute | solution.py:165

commit v2 on v0

v2 whole, which is shorter than its diff:
```python
import functools

import jax
import jax.numpy as jnp
from jax import lax
from jax.experimental import pallas as pl
from jax.experimental.pallas import tpu as pltpu
from jax.sharding import PartitionSpec as P

STATE = 128
GROUPS = 8
AXIS = "ctx"
EPS = 1e-05
VMEM_LIMIT = 16 * 2**20
F32, BF16 = jnp.float32, jnp.bfloat16
WIRE = jnp.float16
PEAK = 4 * 3.0 * 6.0
DT_TOP = 1.3133


def plane_size(n, groups):
    size = 1
    while (2 * size) ** 3 <= 4 * n and n % (2 * size) == 0 and groups % (2 * size) == 0:
        size *= 2
    return size


def silu(v):
    return v / (1.0 + jnp.exp(-v))


def split(v):
    hi = v.astype(BF16)
    return hi, (v - hi.astype(F32)).astype(BF16)


def mm(a, b, dims=((1,), (0,))):
    return lax.dot_general(a, b, (dims, ((), ())), preferred_element_type=F32)


def spread(v, e_ref):
    hi = v.astype(BF16)
    rest = v - hi.astype(F32)
    mid = rest.astype(BF16)
    low = (rest - mid.astype(F32)).astype(BF16)
    return mm(jnp.concatenate([hi, mid, low], axis=1), e_ref[...])


def conv_silu(x, halo, taps):
    count = taps.shape[0]
    xf = x.astype(F32)
    hf = halo.astype(F32)
    at = lax.broadcasted_iota(jnp.int32, (8, 1), 0)
    total = taps[count - 1 : count] * xf
    for back in range(1, count):
        moved = pltpu.roll(xf, back, 0)
        top = moved[:8]
        for row in range(back):
            src = hf.shape[0] - back + row
            top = jnp.where(at == row, hf[src : src + 1], top)
        moved = jnp.concatenate([top, moved[8:]], axis=0)
        total = total + taps[count - 1 - back : count - back] * moved
    return silu(total)


def ends_kernel(x_ref, bc_ref, out_ref):
    count, width = out_ref.shape[0], x_ref.shape[1]
    out_ref[:, :width] = x_ref[8 - count :]
    out_ref[:, width:] = bc_ref[8 - count :]


def load_kernel(*refs):
    count = (len(refs) - 1) // 2
    copies = [pltpu.make_async_copy(refs[k], refs[count + k], refs[-1].at[k]) for k in range(count)]
    for copy in copies:
        copy.start()
    for copy in copies:
        copy.wait()


def steps_kernel(dt_ref, bias_ref, rate_ref, skip_ref, tail_ref, cum_ref, row_ref, ecum_ref, tot_ref):
    groups, rows, per = tail_ref.shape
    v = dt_ref[...].astype(F32) + bias_ref[...]
    dt = jnp.maximum(v, 0.0) + jnp.log1p(jnp.exp(-jnp.abs(v)))
    cum = -rate_ref[...] * dt
    at = lax.broadcasted_iota(jnp.int32, cum.shape, 0)
    step = 1
    while step < rows:
        cum = cum + jnp.where(at >= step, pltpu.roll(cum, step, 0), 0.0)
        step *= 2
    total = cum[rows - 1 : rows]
    tot_ref[...] = total
    tail = jnp.exp(total - cum) * dt
    ecum = jnp.exp(cum)
    row = (jnp.log(dt) - cum).T
    for g in range(groups):
        cols = slice(g * per, (g + 1) * per)
        tail_ref[g] = tail[:, cols]
        cum_ref[g] = cum[:, cols]
        row_ref[g] = row[cols]
        ecum_ref[g, :rows] = ecum[:, cols]
        ecum_ref[g, rows:] = jnp.broadcast_to(skip_ref[:, cols], (8, per))


def reverse(p, bits):
    return sum(((p >> k) & 1) << (bits - 1 - k) for k in range(bits))


def my_place(plane):
    index = lax.axis_index(AXIS)
    return lax.rem(index, plane), lax.div(index, plane)


def rows_kernel(logs_ref, e_ref, tree_ref, chain_ref):
    chunks, plane, _, unit = tree_ref.shape
    bits = plane.bit_length() - 1
    per = e_ref.shape[0] // 3
    j, z = my_place(plane)
    logs = [logs_ref[r : r + 1] for r in range(plane)]
    rows, flags = [], []
    for bit in range(bits):
        own = sum(logs[1 : 1 << bit], logs[0])
        other = sum(logs[(1 << bit) + 1 : 2 << bit], logs[1 << bit])
        up = ((j >> bit) & 1) == 1
        none = jnp.zeros_like(own)
        rows += [
            jnp.where(up, none, other),
            jnp.where(up, own, none),
            jnp.where(up, none, own),
            none,
            jnp.where(up, other, none),
            none,
        ]
        flags += [1.0, 1.0, 1.0, jnp.where(up, 0.0, 1.0), 1.0, jnp.where(up, 1.0, 0.0)]
    rows.append(sum(logs[1:], logs[0]))
    flags.append(1.0)
    rows += [rows[-1]] * (-len(rows) % 8)
    decays = jnp.exp(jnp.concatenate(rows, axis=0))
    wide = [spread(decays[:, g * per : (g + 1) * per], e_ref) for g in range(chunks * plane)]
    for g in range(chunks * plane):
        at = reverse((g // chunks) ^ j, bits)
        for kind in range(6 * bits):
            tree_ref[g % chunks, at, kind : kind + 1] = wide[g][kind : kind + 1] * flags[kind]
    tops = []
    for chunk in range(chunks):
        top = wide[chunk][6 * bits : 6 * bits + 1]
        for q in range(1, plane):
            g = q * chunks + chunk
            top = jnp.where(j == q, wide[g][6 * bits : 6 * bits + 1], top)
        tops.append(top)
    one = jnp.ones((1, unit), F32)
    planes, moves = chain_shape(plane, chunks)
    at = 0
    for step in range(moves):
        total = jnp.zeros_like(one)
        for chunk in range(chunks):
            here = jnp.where(step - z == chunk, 1.0, 0.0)
            total = total + tops[chunk] * here
            chain_ref[at + 1 + chunk] = one * here
        chain_ref[at] = total
        at += 1 + chunks
    for here in range(planes):
        chain_ref[at + here] = one * jnp.where(z == here, 1.0, 0.0)


def chain_shape(plane, chunks):
    planes = lax.axis_size(AXIS) // plane
    return planes, chunks + planes - 2 if planes > 1 else 0


def group_at(p, chunk, chunks, bits):
    return (reverse(p, bits) ^ my_place(1 << bits)[0]) * chunks + chunk


def lanes(at, size):
    return pl.ds(pl.multiple_of(at * size, size), size)


def state_kernel(place, token_ref, x_ref, rim_ref, tx_ref, b_ref, tb_ref, tail_ref, e_ref, s_ref, xc_ref):
    chunk, base, size, chunks, bits = place
    unit = e_ref.shape[1]
    for k in range(size):
        g = group_at(base + k, chunk, chunks, bits)
        at, at_b = lanes(g, unit), lanes(g, STATE)
        at_rim = lanes(g + x_ref.shape[1] // STATE, STATE)
        xc = conv_silu(x_ref[:, at], rim_ref[:, at], tx_ref[:, at])
        xc_ref[k] = xc
        b = conv_silu(b_ref[:, at_b], rim_ref[:, at_rim], tb_ref[:, at_b])
        xt = xc * spread(tail_ref[g], e_ref)
        xhi, xlo = split(xt)
        bhi, blo = split(b)
        s = mm(jnp.concatenate([bhi, blo], axis=0), jnp.concatenate([xhi, xhi], axis=0), ((0,), (0,)))
        s_ref[k] = s + mm(bhi, xlo, ((0,), (0,)))


def local_kernel(place, token_ref, b_ref, rim_ref, tb_ref, xc_ref, cum_ref, row_ref, ecum_ref, e_ref, z_ref, m1_ref, m2_ref, co_ref):
    chunk, base, size, chunks, bits = place
    unit = e_ref.shape[1]
    rows = z_ref.shape[0]
    per = cum_ref.shape[2]
    hdim = unit // per
    causal = lax.broadcasted_iota(jnp.int32, (rows, rows), 0) >= lax.broadcasted_iota(jnp.int32, (rows, rows), 1)
    first = lax.broadcasted_iota(jnp.int32, (rows, 2 * hdim), 1) < hdim
    last = ((1,), (1,))
    for k in range(size):
        g = group_at(base + k, chunk, chunks, bits)
        at = lanes(g, unit)
        pair_bc = []
        for more in (0, GROUPS):
            at_b = lanes(g + more, STATE)
            at_rim = lanes(g + more + z_ref.shape[1] // STATE, STATE)
            pair_bc.append(conv_silu(b_ref[:, at_b], rim_ref[:, at_rim], tb_ref[:, at_b]))
        b, c = pair_bc
        co_ref[k] = c
        bhi, blo = split(b)
        chi, clo = split(c)
        scores = mm(jnp.concatenate([chi, clo], axis=1), jnp.concatenate([bhi, bhi], axis=1), last) + mm(chi, blo, last)
        wide = spread(ecum_ref[g], e_ref)
        z = silu(z_ref[:, at].astype(F32))
        m1_ref[k] = wide[:rows] * z
        skip = wide[rows : rows + 1]
        for pair in range(per // 2):
            cols = slice(pair * 2 * hdim, (pair + 1) * 2 * hdim)
            weights = []
            for h in (2 * pair, 2 * pair + 1):
                e = jnp.exp(cum_ref[g, :, h : h + 1] + row_ref[g, h : h + 1, :])
                weights.append(jnp.where(causal, e * scores, 0.0))
            w = jnp.concatenate(weights, axis=1)
            x = xc_ref[k, :, cols]
            xb = jnp.concatenate([jnp.where(first, x, 0.0), jnp.where(first, 0.0, x)], axis=0)
            whi, wlo = split(w)
            xhi, xlo = split(xb)
            y = mm(whi, xhi) + mm(wlo, xhi) + mm(whi, xlo)
            m2_ref[k, :, cols] = (y + skip[:, cols] * x) * z[:, cols]


def finish_kernel(place, token_ref, p_ref, c_ref, m1_ref, m2_ref, gain_ref, *refs):
    chunk, base, size, chunks, bits = place
    out_ref, done_ref, sem = refs[-3:]
    unit = p_ref.shape[2]
    copies = []
    for k in range(size):
        at = lanes(group_at(base + k, chunk, chunks, bits), unit)
        chi, clo = split(c_ref[k])
        phi, plo = split(p_ref[k])
        y = mm(jnp.concatenate([chi, clo], axis=1), jnp.concatenate([phi, phi], axis=0)) + mm(chi, plo)
        gated = m2_ref[k] + m1_ref[k] * y
        scale = lax.rsqrt(jnp.mean(gated * gated, axis=1, keepdims=True) + EPS)
        done_ref[k] = (gated * scale * gain_ref[:, at]).astype(BF16)
        copies.append(pltpu.make_async_copy(done_ref.at[k], out_ref.at[:, at], sem.at[k]))
        copies[-1].start()
    for copy in copies:
        copy.wait()


def shards(x_in, bc_in, z_in, dt_in, conv_x, conv_bc, dt_bias, a_rate, d_skip, gain):
    rows, width = x_in.shape
    heads = dt_bias.shape[0]
    hdim = width // heads
    per = heads // GROUPS
    unit = per * hdim
    gain = gain[None]
    x_in, bc_in, z_in, conv_x, conv_bc, gain = [
        pltpu.with_memory_space_constraint(v, pltpu.HBM) for v in (x_in, bc_in, z_in, conv_x, conv_bc, gain)
    ]
    count = conv_x.shape[0]
    axis = AXIS
    n = lax.axis_size(axis)
    plane = plane_size(n, GROUPS)
    planes = n // plane
    chunks = GROUPS // plane
    bits = plane.bit_length() - 1
    half = plane // 2
    scale = 2.0 ** -max(0, 1 + int(n * rows * DT_TOP * PEAK * PEAK / 65504.0).bit_length())
    small_vmem = pltpu.CompilerParams(vmem_limit_bytes=VMEM_LIMIT)
    in_vmem = pl.BlockSpec(memory_space=pltpu.VMEM)
    in_hbm = pl.BlockSpec(memory_space=pltpu.HBM)

    def near(v):
        return pltpu.with_memory_space_constraint(v, pltpu.VMEM)

    def swap(v, bit):
        return lax.ppermute(v, axis, [(i, i ^ (1 << bit)) for i in range(n)])

    def pack(v):
        return (v * scale).astype(WIRE)

    def unpack(v):
        return v.astype(F32) * (1.0 / scale)

    last = rows // 8 - 1
    ends = pl.pallas_call(
        ends_kernel,
        grid=(1,),
        out_shape=jax.ShapeDtypeStruct((count - 1, width + bc_in.shape[1]), BF16),
        in_specs=[
            pl.BlockSpec((8, width), lambda s: (last, 0)),
            pl.BlockSpec((8, bc_in.shape[1]), lambda s: (last, 0)),
        ],
        out_specs=pl.BlockSpec((count - 1, width + bc_in.shape[1]), lambda s: (0, 0)),
        compiler_params=small_vmem,
    )(x_in, bc_in)
    rim = near(lax.ppermute(ends, axis, [(i, i + 1) for i in range(n - 1)]))
    held = (x_in, bc_in, z_in, conv_x, conv_bc, gain)
    x_in, bc_in, z_in, conv_x, conv_bc, gain = pl.pallas_call(
        load_kernel,
        out_shape=[pltpu.VMEM(v.shape, v.dtype) for v in held],
        in_specs=[pl.BlockSpec(memory_space=pltpu.HBM)] * len(held),
        out_specs=[in_vmem] * len(held),
        scratch_shapes=[pltpu.SemaphoreType.DMA((len(held),))],
        compiler_params=small_vmem,
    )(*held)

    small = [
        pltpu.VMEM((GROUPS, rows, per), F32),
        pltpu.VMEM((GROUPS, rows, per), F32),
        pltpu.VMEM((GROUPS, per, rows), F32),
        pltpu.VMEM((GROUPS, rows + 8, per), F32),
        jax.ShapeDtypeStruct((1, heads), F32),
    ]
    tail, cum, row, ecum, total = pl.pallas_call(
        steps_kernel,
        out_shape=small,
        out_specs=[in_vmem] * len(small),
        compiler_params=small_vmem,
    )(dt_in, dt_bias[None], a_rate[None], d_skip[None])
    token = near(total)
    logs = total
    for bit in range(bits):
        logs = jnp.concatenate([logs, swap(logs, bit)], axis=0)

    head_map = (jnp.arange(unit)[None, :] // hdim == jnp.arange(per)[:, None]).astype(BF16)
    head_map = near(jnp.concatenate([head_map] * 3, axis=0))
    moves = chain_shape(plane, chunks)[1]
    tree, chain = pl.pallas_call(
        rows_kernel,
        out_shape=[
            pltpu.VMEM((chunks, plane, 6 * bits, unit), F32),
            pltpu.VMEM((moves * (1 + chunks) + planes, 1, unit), F32),
        ],
        in_specs=[in_vmem] * 2,
        out_specs=[in_vmem] * 2,
        compiler_params=small_vmem,
    )(near(logs), head_map)

    def factor(chunk, size, bit, kind):
        return tree[chunk, :size, 6 * bit + kind][:, None]

    def tie(value, *others):
        return lax.optimization_barrier((value, *others))[0] if others else value

    def call(body, place, outs, args, after):
        return pl.pallas_call(
            functools.partial(body, (*place, chunks, bits)),
            out_shape=[pltpu.VMEM(*o) for o in outs],
            in_specs=[in_vmem] * (1 + len(args)),
            out_specs=[in_vmem] * len(outs),
            compiler_params=small_vmem,
        )(tie(token, *after), *args)

    def states(*place, after=()):
        size = place[2]
        outs = [((size, STATE, unit), F32), ((size, rows, unit), F32)]
        return call(state_kernel, place, outs, (x_in, rim, conv_x, bc_in, conv_bc, tail, head_map), after)

    def local(*place, xc, after=()):
        size = place[2]
        outs = [((size, rows, unit), F32)] * 2 + [((size, rows, STATE), F32)]
        return call(local_kernel, place, outs, (bc_in, rim, conv_bc, xc, cum, row, ecum, head_map, z_in), after)

    def finish(*place, before, mixed, out):
        size = place[2]
        m1, m2, c = mixed
        kept = () if out is None else (out,)
        return pl.pallas_call(
            functools.partial(finish_kernel, (*place, chunks, bits)),
            out_shape=jax.ShapeDtypeStruct((rows, width), BF16),
            in_specs=[in_vmem] * 6 + [in_hbm] * len(kept),
            out_specs=in_hbm,
            scratch_shapes=[pltpu.VMEM((size, rows, unit), BF16), pltpu.SemaphoreType.DMA((size,))],
            input_output_aliases={6: 0} if kept else {},
            compiler_params=small_vmem,
        )(token, near(before), c, m1, m2, gain, *kept)

    levels = [[] for _ in range(chunks)]
    tops, pieces = [], []

    def climb(chunk, keep, wire, bit):
        levels[chunk].append((keep, wire))
        size = keep.shape[0]
        return keep * factor(chunk, size, bit, 0) + unpack(wire) * factor(chunk, size, bit, 1)

    gate = ()
    for chunk in range(chunks):
        s_far, xc_far = states(chunk, half, half, after=gate)
        give = pack(s_far)
        wire = swap(give, 0)
        s_near, xc_near = states(chunk, 0, half, after=(give,))
        pieces += [(chunk, half, xc_far), (chunk, 0, xc_near)]
        both = climb(chunk, s_near, wire, 0)
        for bit in range(1, bits):
            cut = both.shape[0] // 2
            keep, give = both[:cut], pack(both[cut:])
            gate = (give,)
            both = climb(chunk, keep, swap(give, bit), bit)
        tops.append(lax.optimization_barrier(both))

    pairs = [(i, i + plane) for i in range(n - plane)]
    entering = [jnp.zeros((1, STATE, unit), WIRE)]
    mixes = {}

    def work(number, *after):
        for _ in range(number):
            if len(mixes) < len(pieces):
                chunk, base, xc = pieces[len(mixes)]
                mixes[chunk, base] = local(chunk, base, half, xc=xc, after=after)

    for step in range(moves):
        at = step * (1 + chunks)
        value = unpack(entering[-1]) * chain[at] if step else 0.0
        for chunk in range(max(0, step - planes + 1), min(chunks - 1, step) + 1):
            value = value + tops[chunk] * chain[at + 1 + chunk]
        give = pack(value)
        wire = lax.ppermute(give, axis, pairs)
        if step:
            done = len(mixes)
            work(1, give)
            if len(mixes) > done:
                wire = tie(wire, list(mixes.values())[-1][2])
        entering.append(wire)
    work(len(pieces))

    out = None
    for chunk in range(chunks):
        state = 0.0
        for at in range(1, planes):
            if chunk + at < len(entering):
                state = state + unpack(entering[chunk + at]) * chain[moves * (1 + chunks) + at]
        other = None
        for bit in reversed(range(bits)):
            keep, got = levels[chunk][bit]
            size = keep.shape[0]
            give = pack(state * factor(chunk, size, bit, 2) + keep * factor(chunk, size, bit, 3))
            other = unpack(swap(give, bit))
            state = state * factor(chunk, size, bit, 4) + unpack(got) * factor(chunk, size, bit, 5)
            if bit:
                state = jnp.concatenate([state, other], axis=0)
        out = finish(chunk, 0, half, before=state, mixed=mixes[chunk, 0], out=out)
        out = finish(chunk, half, half, before=other, mixed=mixes[chunk, half], out=out)
    return out


def solution(mesh):
    split_rows = P(("groups", "ctx"), None)
    return jax.shard_map(
        shards,
        mesh=mesh,
        in_specs=(split_rows,) * 4 + (P(),) * 6,
        out_specs=split_rows,
        check_vma=False,
    )
```

time: 355 us -> 81.3 us (0.23)
  waiting for transfers between devices: 183 us -> 18.2 us
  other arithmetic: 58.5 us -> 3.27 us
  local copies, waits for them, and re-layouts: 55.6 us -> 2.78 us
  matrix products: 30.1 us -> 0 us
  Pallas kernels: 0 us -> 25.1 us
  starting transfers between devices: 22.3 us -> 30.3 us
    all_to_all x3 -> x0, waiting for transfers between devices: 183 us -> none  [the longest x1 91.7 us: shards(): lax.all_to_all(flat, 'ctx', split_axis=1, concat_axis=0, tiled=True)]
    dot_general x4 -> x0, matrix products: 30.1 us -> none  [the longest x1 18.1 us: block_terms(): y_diag = jnp.einsum('gkts,sgkp->tgkp', weights, xg, precision=HIGH)]
    ppermute x1 -> x15, starting transfers between devices: 3.54 us -> 30.3 us  [the longest x10 14.1 us: swap(): return lax.ppermute(v, axis, [(i, i ^ 1 << bit) for i in range(n)])]
    pallas_call x0 -> x16, Pallas kernels: none -> 25.1 us  [the longest x8 15.3 us: call(): pl.pallas_call(functools.partial(body, (*place, chunks, bits)), out_shape...]
    all_to_all x3 -> x0, starting transfers between devices: 18.7 us -> none  [the longest x1 6.94 us: shards(): lax.all_to_all(flat, 'ctx', split_axis=1, concat_axis=0, tiled=True)]
    unnamed x40 -> x14, local copies, waits for them, and re-layouts: 21 us -> 2.78 us
    ppermute x1 -> x15, waiting for transfers between devices: 0.39 us -> 18.2 us  [the longest x10 10.9 us: swap(): return lax.ppermute(v, axis, [(i, i ^ 1 << bit) for i in range(n)])]
    mul x6 -> x5, other arithmetic: 15.4 us -> 0.36 us  [the longest x4 0.33 us: unpack(): return v.astype(F32) * (1.0 / scale)]
  transfers between devices with their start and end apart: 4 -> 15, of which waited for: 3 -> 8; matrix products, arithmetic and copies ran while one was open for 13% -> 2% of each run, Pallas kernels for 0% -> 27%
where the time goes in v2:
time: 81.3 us; the launch traced here: 80.2 us
  starting transfers between devices  30.3 us (37%)
  Pallas kernels  25.1 us (31%)
  waiting for transfers between devices  18.2 us (22%)
  other arithmetic  3.27 us (4%)
  local copies, waits for them, and re-layouts  2.78 us (3%)
    pallas_call x8, Pallas kernels, call(): pl.pallas_call(functools.partial(body, (*place, chunks, bits)), out_shape...  15.3 us
    ppermute x10, starting transfers between devices, swap(): return lax.ppermute(v, axis, [(i, i ^ 1 << bit) for i in range(n)])  14.1 us
    ppermute x4, starting transfers between devices, shards(): wire = lax.ppermute(give, axis, pairs)  13 us
    ppermute x10, waiting for transfers between devices, swap(): return lax.ppermute(v, axis, [(i, i ^ 1 << bit) for i in range(n)])  10.9 us
    ppermute x4, waiting for transfers between devices, shards(): wire = lax.ppermute(give, axis, pairs)  7.38 us
    pallas_call x4, Pallas kernels, finish(): pl.pallas_call(functools.partial(finish_kernel, (*place, chunks, bits)),...  5.46 us
    ppermute x1, starting transfers between devices, shards(): rim = near(lax.ppermute(ends, axis, [(i, i + 1) for i in range(n - 1)]))  3.08 us
    unnamed x14, local copies, waits for them, and re-layouts  2.78 us
  transfers between devices with their start and end apart: 15, of which 8 were waited for; matrix products, arithmetic and copies ran while one was open for 2% of the time, Pallas kernels for 27%

profile of v2, /device:TPU:11, one launch (start us, length us, event | category | flops | bytes accessed | tf_op | source)
XLA Modules:
  0.0 80.2 jit_solution(5055058622144218235)
XLA Ops:
  4.9 3.1 %collective-permute-start = (bf16[3,10240]{1,0:T(4,128)(2,1)S(1)}, bf16[3,10240]{1,0:T(4,128)(2,1)S(1)}, u32[]{:S(2)}, u32[]{:S(2)}) collective-permute-start(bf16[3,10240]{1,0:T(4,128)(2,1)S(1)} %shard_map.102), channel_id=1, source_target_pairs={{0,1},{1,2},{2,3},{3,4},{4,5},{5,6},{6,7},{7,8},{8,9},{9,10},{10,1... | collective-permute-start | bytes 184328 | tf_op jit(solution)/shard_map/ppermute | solution.py:303
  8.1 2.4 %shard_map.101 = (bf16[128,8192]{1,0:T(8,128)(2,1)S(1)}, bf16[128,2048]{1,0:T(8,128)(2,1)S(1)}, bf16[128,8192]{1,0:T(8,128)(2,1)S(1)}, f32[4,8192]{1,0:T(4,128)S...) custom-call(bf16[128,8192]{1,0:T(8,128)(2,1)} %x_ref.1, bf16[128,2048]{1,0:T(8,128)(2,1)} %bc_ref.1, ...), custom_call_target="tpu_custom_call" | custom-call | tf_op jit(solution)/shard_map/pallas_call | solution.py:305
  10.8 1.6 %shard_map.103 = (f32[2,128,1024]{2,1,0:T(8,128)S(1)}, f32[2,128,1024]{2,1,0:T(8,128)S(1)}) custom-call(f32[1,128]{1,0:T(1,128)S(1)} %get-tuple-element.74.token_ref, bf16[128,8192]{1,0:T(8,128)(2,1)S(1)} %get-tuple-element.48.x_ref, bf16[3,10240]{1,0:T(4,128)(2,1)S(1)} %collective-permute-done.rim_ref, f32[4,8192]{1,0:T(4,128)S(1)} %get-tuple-element.49.tx_ref, ...), custom_call_target="tpu_custom_call" | custom-call | tf_op jit(solution)/shard_map/pallas_call | solution.py:353
  13.7 1.6 %shard_map.104 = (f32[2,128,1024]{2,1,0:T(8,128)S(1)}, f32[2,128,1024]{2,1,0:T(8,128)S(1)}) custom-call(f32[1,128]{1,0:T(1,128)S(1)} %get-tuple-element.74.token_ref, bf16[128,8192]{1,0:T(8,128)(2,1)S(1)} %get-tuple-element.48.x_ref, bf16[3,10240]{1,0:T(4,128)(2,1)S(1)} %collective-permute-done.rim_ref, f32[4,8192]{1,0:T(4,128)S(1)} %get-tuple-element.49.tx_ref, ...), custom_call_target="tpu_custom_call" | custom-call | tf_op jit(solution)/shard_map/pallas_call | solution.py:353
  15.5 1.6 %shard_map.106 = (f32[2,128,1024]{2,1,0:T(8,128)S(1)}, f32[2,128,1024]{2,1,0:T(8,128)S(1)}) custom-call(f32[1,128]{1,0:T(1,128)S(1)} %get-tuple-element.74.token_ref, bf16[128,8192]{1,0:T(8,128)(2,1)S(1)} %get-tuple-element.48.x_ref, bf16[3,10240]{1,0:T(4,128)(2,1)S(1)} %collective-permute-done.rim_ref, f32[4,8192]{1,0:T(4,128)S(1)} %get-tuple-element.49.tx_ref, ...), custom_call_target="tpu_custom_call" | custom-call | tf_op jit(solution)/shard_map/pallas_call | solution.py:353
  18.7 1.6 %shard_map.107 = (f32[2,128,1024]{2,1,0:T(8,128)S(1)}, f32[2,128,1024]{2,1,0:T(8,128)S(1)}) custom-call(f32[1,128]{1,0:T(1,128)S(1)} %get-tuple-element.74.token_ref, bf16[128,8192]{1,0:T(8,128)(2,1)S(1)} %get-tuple-element.48.x_ref, bf16[3,10240]{1,0:T(4,128)(2,1)S(1)} %collective-permute-done.rim_ref, f32[4,8192]{1,0:T(4,128)S(1)} %get-tuple-element.49.tx_ref, ...), custom_call_target="tpu_custom_call" | custom-call | tf_op jit(solution)/shard_map/pallas_call | solution.py:353
  21.2 4.4 %collective-permute-done.4 = f16[1,128,1024]{2,1,0:T(8,128)(2,1)S(1)} collective-permute-done((f16[1,128,1024]{2,1,0:T(8,128)(2,1)S(1)}, f16[1,128,1024]{2,1,0:T(8,128)(2,1)S(1)}, u32[]{:S(2)}, u32[]{:S(2)}) %collective-permute-start.4) | collective-permute-done | bytes 262176 | tf_op jit(solution)/shard_map/ppermute | solution.py:283
  25.8 3.2 %collective-permute-start.5 = (f16[1,128,1024]{2,1,0:T(8,128)(2,1)S(1)}, f16[1,128,1024]{2,1,0:T(8,128)(2,1)S(1)}, u32[]{:S(2)}, u32[]{:S(2)}) collective-permute-start(f16[1,128,1024]{2,1,0:T(8,128)(2,1)S(1)} %multiply_convert_fusion.6), channel_id=1, source_target_pairs={{0,4},{1,5},{2,6},{3,7},{4,8},{5,9},{6,10},{7,11},{8,12},{9,13},{1... | collective-permute-start | bytes 786440 | tf_op jit(solution)/shard_map/ppermute | solution.py:424
  29.0 2.2 %collective-permute-done.7 = f16[1,128,1024]{2,1,0:T(8,128)(2,1)S(1)} collective-permute-done((f16[1,128,1024]{2,1,0:T(8,128)(2,1)S(1)}, f16[1,128,1024]{2,1,0:T(8,128)(2,1)S(1)}, u32[]{:S(2)}, u32[]{:S(2)}) %collective-permute-start.7) | collective-permute-done | bytes 262176 | tf_op jit(solution)/shard_map/ppermute | solution.py:283
  31.3 2.7 %collective-permute-done.5 = f16[1,128,1024]{2,1,0:T(8,128)(2,1)S(1)} collective-permute-done((f16[1,128,1024]{2,1,0:T(8,128)(2,1)S(1)}, f16[1,128,1024]{2,1,0:T(8,128)(2,1)S(1)}, u32[]{:S(2)}, u32[]{:S(2)}) %collective-permute-start.5) | collective-permute-done | bytes 262176 | tf_op jit(solution)/shard_map/ppermute | solution.py:424
  34.2 3.2 %collective-permute-start.8 = (f16[1,128,1024]{2,1,0:T(8,128)(2,1)S(1)}, f16[1,128,1024]{2,1,0:T(8,128)(2,1)S(1)}, u32[]{:S(2)}, u32[]{:S(2)}) collective-permute-start(f16[1,128,1024]{2,1,0:T(8,128)(2,1)S(1)} %fusion.9), channel_id=1, source_target_pairs={{0,4},{1,5},{2,6},{3,7},{4,8},{5,9},{6,10},{7,11},{8,12},{9,13},{1... | collective-permute-start | bytes 786440 | tf_op jit(solution)/shard_map/ppermute | solution.py:424
  37.4 2.2 %shard_map.108 = (f32[2,128,1024]{2,1,0:T(8,128)S(1)}, f32[2,128,1024]{2,1,0:T(8,128)S(1)}, f32[2,128,128]{2,1,0:T(8,128)S(1)}) custom-call(f32[1,128]{1,0:T(1,128)S(1)} %get-tuple-element.74.token_ref, bf16[128,2048]{1,0:T(8,128)(2,1)S(1)} %get-tuple-element.50.b_ref, bf16[3,10240]{1,0:T(4,128)(2,1)S(1)} %collective-permute-done.rim_ref, ...), custom_call_target="tpu_custom_call" | custom-call | tf_op jit(solution)/shard_map/pallas_call | solution.py:353
  39.6 1.7 %collective-permute-done.8 = f16[1,128,1024]{2,1,0:T(8,128)(2,1)S(1)} collective-permute-done((f16[1,128,1024]{2,1,0:T(8,128)(2,1)S(1)}, f16[1,128,1024]{2,1,0:T(8,128)(2,1)S(1)}, u32[]{:S(2)}, u32[]{:S(2)}) %collective-permute-start.8) | collective-permute-done | bytes 262176 | tf_op jit(solution)/shard_map/ppermute | solution.py:424
  41.5 3.4 %collective-permute-start.9 = (f16[1,128,1024]{2,1,0:T(8,128)(2,1)S(1)}, f16[1,128,1024]{2,1,0:T(8,128)(2,1)S(1)}, u32[]{:S(2)}, u32[]{:S(2)}) collective-permute-start(f16[1,128,1024]{2,1,0:T(8,128)(2,1)S(1)} %fusion.19), channel_id=1, source_target_pairs={{0,4},{1,5},{2,6},{3,7},{4,8},{5,9},{6,10},{7,11},{8,12},{9,13},{1... | collective-permute-start | bytes 786440 | tf_op jit(solution)/shard_map/ppermute | solution.py:424
  44.8 2.2 %shard_map.109 = (f32[2,128,1024]{2,1,0:T(8,128)S(1)}, f32[2,128,1024]{2,1,0:T(8,128)S(1)}, f32[2,128,128]{2,1,0:T(8,128)S(1)}) custom-call(f32[1,128]{1,0:T(1,128)S(1)} %get-tuple-element.74.token_ref, bf16[128,2048]{1,0:T(8,128)(2,1)S(1)} %get-tuple-element.50.b_ref, bf16[3,10240]{1,0:T(4,128)(2,1)S(1)} %collective-permute-done.rim_ref, ...), custom_call_target="tpu_custom_call" | custom-call | tf_op jit(solution)/shard_map/pallas_call | solution.py:353
  47.1 1.5 %collective-permute-done.9 = f16[1,128,1024]{2,1,0:T(8,128)(2,1)S(1)} collective-permute-done((f16[1,128,1024]{2,1,0:T(8,128)(2,1)S(1)}, f16[1,128,1024]{2,1,0:T(8,128)(2,1)S(1)}, u32[]{:S(2)}, u32[]{:S(2)}) %collective-permute-start.9) | collective-permute-done | bytes 262176 | tf_op jit(solution)/shard_map/ppermute | solution.py:424
  48.8 3.3 %collective-permute-start.10 = (f16[1,128,1024]{2,1,0:T(8,128)(2,1)S(1)}, f16[1,128,1024]{2,1,0:T(8,128)(2,1)S(1)}, u32[]{:S(2)}, u32[]{:S(2)}) collective-permute-start(f16[1,128,1024]{2,1,0:T(8,128)(2,1)S(1)} %fusion.23), channel_id=1, source_target_pairs={{0,4},{1,5},{2,6},{3,7},{4,8},{5,9},{6,10},{7,11},{8,12},{9,13},{1... | collective-permute-start | bytes 786440 | tf_op jit(solution)/shard_map/ppermute | solution.py:424
  52.1 2.2 %shard_map.110 = (f32[2,128,1024]{2,1,0:T(8,128)S(1)}, f32[2,128,1024]{2,1,0:T(8,128)S(1)}, f32[2,128,128]{2,1,0:T(8,128)S(1)}) custom-call(f32[1,128]{1,0:T(1,128)S(1)} %get-tuple-element.74.token_ref, bf16[128,2048]{1,0:T(8,128)(2,1)S(1)} %get-tuple-element.50.b_ref, bf16[3,10240]{1,0:T(4,128)(2,1)S(1)} %collective-permute-done.rim_ref, ...), custom_call_target="tpu_custom_call" | custom-call | tf_op jit(solution)/shard_map/pallas_call | solution.py:353
  54.3 1.5 %collective-permute-done.10 = f16[1,128,1024]{2,1,0:T(8,128)(2,1)S(1)} collective-permute-done((f16[1,128,1024]{2,1,0:T(8,128)(2,1)S(1)}, f16[1,128,1024]{2,1,0:T(8,128)(2,1)S(1)}, u32[]{:S(2)}, u32[]{:S(2)}) %collective-permute-start.10) | collective-permute-done | bytes 262176 | tf_op jit(solution)/shard_map/ppermute | solution.py:424
  56.5 1.6 %collective-permute-start.13 = (f16[1,128,1024]{2,1,0:T(8,128)(2,1)S(1)}, f16[1,128,1024]{2,1,0:T(8,128)(2,1)S(1)}, u32[]{:S(2)}, u32[]{:S(2)}) collective-permute-start(f16[1,128,1024]{2,1,0:T(8,128)(2,1)S(1)} %get-tuple-element.94), channel_id=1, source_target_pairs={{0,2},{1,3},{2,0},{3,1},{4,6},{5,7},{6,4},{7,5},{8,10},{9,11},{10,... | collective-permute-start | bytes 786440 | tf_op jit(solution)/shard_map/ppermute | solution.py:283
  58.2 3.6 %collective-permute-done.13 = f16[1,128,1024]{2,1,0:T(8,128)(2,1)S(1)} collective-permute-done((f16[1,128,1024]{2,1,0:T(8,128)(2,1)S(1)}, f16[1,128,1024]{2,1,0:T(8,128)(2,1)S(1)}, u32[]{:S(2)}, u32[]{:S(2)}) %collective-permute-start.13) | collective-permute-done | bytes 262176 | tf_op jit(solution)/shard_map/ppermute | solution.py:283
  62.3 7.0 %collective-permute-start.14 = (f16[2,128,1024]{2,1,0:T(8,128)(2,1)S(1)}, f16[2,128,1024]{2,1,0:T(8,128)(2,1)S(1)}, u32[]{:S(2)}, u32[]{:S(2)}) collective-permute-start(f16[2,128,1024]{2,1,0:T(8,128)(2,1)S(1)} %get-tuple-element.90), channel_id=1, source_target_pairs={{0,1},{1,0},{2,3},{3,2},{4,5},{5,4},{6,7},{7,6},{8,9},{9,8},{10,11... | collective-permute-start | bytes 1572872 | tf_op jit(solution)/shard_map/ppermute | solution.py:283
  69.7 2.3 %collective-permute-start.12 = (f16[2,128,1024]{2,1,0:T(8,128)(2,1)S(1)}, f16[2,128,1024]{2,1,0:T(8,128)(2,1)S(1)}, u32[]{:S(2)}, u32[]{:S(2)}) collective-permute-start(f16[2,128,1024]{2,1,0:T(8,128)(2,1)S(1)} %get-tuple-element.92), channel_id=1, source_target_pairs={{0,1},{1,0},{2,3},{3,2},{4,5},{5,4},{6,7},{7,6},{8,9},{9,8},{10,11... | collective-permute-start | bytes 1572872 | tf_op jit(solution)/shard_map/ppermute | solution.py:283
  72.0 2.2 %shard_map.111 = (f32[2,128,1024]{2,1,0:T(8,128)S(1)}, f32[2,128,1024]{2,1,0:T(8,128)S(1)}, f32[2,128,128]{2,1,0:T(8,128)S(1)}) custom-call(f32[1,128]{1,0:T(1,128)S(1)} %get-tuple-element.74.token_ref, bf16[128,2048]{1,0:T(8,128)(2,1)S(1)} %get-tuple-element.50.b_ref, bf16[3,10240]{1,0:T(4,128)(2,1)S(1)} %collective-permute-done.rim_ref, ...), custom_call_target="tpu_custom_call" | custom-call | tf_op jit(solution)/shard_map/pallas_call | solution.py:353
  (63 shorter events, 17.2 us)
Async XLA Ops:
  0.0 0.8 copy-start
  0.8 0.7 copy-start.1
  1.4 0.7 copy-start.2
  2.1 0.7 copy-start.3
  3.3 7.3 %collective-permute-start.1 = (f32[1,128]{1,0:T(1,128)S(1)}, f32[1,128]{1,0:T(1,128)S(1)}, u32[]{:S(2)}, u32[]{:S(2)}) collective-permute-start(f32[1,128]{1,0:T(1,128)S(1)} %get-tuple-element.74.token_ref), channel_id=1, source_target_pairs={{0,1},{1,0},{2,3},{3,2},{4,5},{5,4},{6,7},{7,6},{8,9},{9,8},{10,11... | collective-permute-start | bytes 1544 | tf_op jit(solution)/shard_map/ppermute | solution.py:283
  4.9 5.9 %collective-permute-start = (bf16[3,10240]{1,0:T(4,128)(2,1)S(1)}, bf16[3,10240]{1,0:T(4,128)(2,1)S(1)}, u32[]{:S(2)}, u32[]{:S(2)}) collective-permute-start(bf16[3,10240]{1,0:T(4,128)(2,1)S(1)} %shard_map.102), channel_id=1, source_target_pairs={{0,1},{1,2},{2,3},{3,4},{4,5},{5,6},{6,7},{7,8},{8,9},{9,10},{10,1... | collective-permute-start | bytes 184328 | tf_op jit(solution)/shard_map/ppermute | solution.py:303
  10.6 2.6 %collective-permute-start.2 = (f32[2,128]{1,0:T(2,128)S(1)}, f32[2,128]{1,0:T(2,128)S(1)}, u32[]{:S(2)}, u32[]{:S(2)}) collective-permute-start(f32[2,128]{1,0:T(2,128)S(1)} %pad_maximum_fusion.3), channel_id=1, source_target_pairs={{0,2},{1,3},{2,0},{3,1},{4,6},{5,7},{6,4},{7,5},{8,10},{9,11},{10,... | collective-permute-start | bytes 3080 | tf_op jit(solution)/shard_map/ppermute | solution.py:283
  12.5 2.8 %collective-permute-start.3 = (f16[2,128,1024]{2,1,0:T(8,128)(2,1)S(1)}, f16[2,128,1024]{2,1,0:T(8,128)(2,1)S(1)}, u32[]{:S(2)}, u32[]{:S(2)}) collective-permute-start(f16[2,128,1024]{2,1,0:T(8,128)(2,1)S(1)} %multiply_convert_fusion.3), channel_id=1, source_target_pairs={{0,1},{1,0},{2,3},{3,2},{4,5},{5,4},{6,7},{7,6},{8,9},{9,8},{10,11... | collective-permute-start | bytes 1572872 | tf_op jit(solution)/shard_map/ppermute | solution.py:283
  17.2 3.0 %collective-permute-start.6 = (f16[2,128,1024]{2,1,0:T(8,128)(2,1)S(1)}, f16[2,128,1024]{2,1,0:T(8,128)(2,1)S(1)}, u32[]{:S(2)}, u32[]{:S(2)}) collective-permute-start(f16[2,128,1024]{2,1,0:T(8,128)(2,1)S(1)} %multiply_convert_fusion.2), channel_id=1, source_target_pairs={{0,1},{1,0},{2,3},{3,2},{4,5},{5,4},{6,7},{7,6},{8,9},{9,8},{10,11... | collective-permute-start | bytes 1572872 | tf_op jit(solution)/shard_map/ppermute | solution.py:283
  17.8 7.8 %collective-permute-start.4 = (f16[1,128,1024]{2,1,0:T(8,128)(2,1)S(1)}, f16[1,128,1024]{2,1,0:T(8,128)(2,1)S(1)}, u32[]{:S(2)}, u32[]{:S(2)}) collective-permute-start(f16[1,128,1024]{2,1,0:T(8,128)(2,1)S(1)} %fusion.25), channel_id=1, source_target_pairs={{0,2},{1,3},{2,0},{3,1},{4,6},{5,7},{6,4},{7,5},{8,10},{9,11},{10,... | collective-permute-start | bytes 786440 | tf_op jit(solution)/shard_map/ppermute | solution.py:283
  20.5 10.7 %collective-permute-start.7 = (f16[1,128,1024]{2,1,0:T(8,128)(2,1)S(1)}, f16[1,128,1024]{2,1,0:T(8,128)(2,1)S(1)}, u32[]{:S(2)}, u32[]{:S(2)}) collective-permute-start(f16[1,128,1024]{2,1,0:T(8,128)(2,1)S(1)} %fusion.24), channel_id=1, source_target_pairs={{0,2},{1,3},{2,0},{3,1},{4,6},{5,7},{6,4},{7,5},{8,10},{9,11},{10,... | collective-permute-start | bytes 786440 | tf_op jit(solution)/shard_map/ppermute | solution.py:283
  25.8 8.2 %collective-permute-start.5 = (f16[1,128,1024]{2,1,0:T(8,128)(2,1)S(1)}, f16[1,128,1024]{2,1,0:T(8,128)(2,1)S(1)}, u32[]{:S(2)}, u32[]{:S(2)}) collective-permute-start(f16[1,128,1024]{2,1,0:T(8,128)(2,1)S(1)} %multiply_convert_fusion.6), channel_id=1, source_target_pairs={{0,4},{1,5},{2,6},{3,7},{4,8},{5,9},{6,10},{7,11},{8,12},{9,13},{1... | collective-permute-start | bytes 786440 | tf_op jit(solution)/shard_map/ppermute | solution.py:424
  34.2 7.1 %collective-permute-start.8 = (f16[1,128,1024]{2,1,0:T(8,128)(2,1)S(1)}, f16[1,128,1024]{2,1,0:T(8,128)(2,1)S(1)}, u32[]{:S(2)}, u32[]{:S(2)}) collective-permute-start(f16[1,128,1024]{2,1,0:T(8,128)(2,1)S(1)} %fusion.9), channel_id=1, source_target_pairs={{0,4},{1,5},{2,6},{3,7},{4,8},{5,9},{6,10},{7,11},{8,12},{9,13},{1... | collective-permute-start | bytes 786440 | tf_op jit(solution)/shard_map/ppermute | solution.py:424
  41.5 7.1 %collective-permute-start.9 = (f16[1,128,1024]{2,1,0:T(8,128)(2,1)S(1)}, f16[1,128,1024]{2,1,0:T(8,128)(2,1)S(1)}, u32[]{:S(2)}, u32[]{:S(2)}) collective-permute-start(f16[1,128,1024]{2,1,0:T(8,128)(2,1)S(1)} %fusion.19), channel_id=1, source_target_pairs={{0,4},{1,5},{2,6},{3,7},{4,8},{5,9},{6,10},{7,11},{8,12},{9,13},{1... | collective-permute-start | bytes 786440 | tf_op jit(solution)/shard_map/ppermute | solution.py:424
  48.8 7.1 %collective-permute-start.10 = (f16[1,128,1024]{2,1,0:T(8,128)(2,1)S(1)}, f16[1,128,1024]{2,1,0:T(8,128)(2,1)S(1)}, u32[]{:S(2)}, u32[]{:S(2)}) collective-permute-start(f16[1,128,1024]{2,1,0:T(8,128)(2,1)S(1)} %fusion.23), channel_id=1, source_target_pairs={{0,4},{1,5},{2,6},{3,7},{4,8},{5,9},{6,10},{7,11},{8,12},{9,13},{1... | collective-permute-start | bytes 786440 | tf_op jit(solution)/shard_map/ppermute | solution.py:424
  56.5 5.3 %collective-permute-start.13 = (f16[1,128,1024]{2,1,0:T(8,128)(2,1)S(1)}, f16[1,128,1024]{2,1,0:T(8,128)(2,1)S(1)}, u32[]{:S(2)}, u32[]{:S(2)}) collective-permute-start(f16[1,128,1024]{2,1,0:T(8,128)(2,1)S(1)} %get-tuple-element.94), channel_id=1, source_target_pairs={{0,2},{1,3},{2,0},{3,1},{4,6},{5,7},{6,4},{7,5},{8,10},{9,11},{10,... | collective-permute-start | bytes 786440 | tf_op jit(solution)/shard_map/ppermute | solution.py:283
  58.1 11.2 %collective-permute-start.11 = (f16[1,128,1024]{2,1,0:T(8,128)(2,1)S(1)}, f16[1,128,1024]{2,1,0:T(8,128)(2,1)S(1)}, u32[]{:S(2)}, u32[]{:S(2)}) collective-permute-start(f16[1,128,1024]{2,1,0:T(8,128)(2,1)S(1)} %get-tuple-element.97), channel_id=1, source_target_pairs={{0,2},{1,3},{2,0},{3,1},{4,6},{5,7},{6,4},{7,5},{8,10},{9,11},{10,... | collective-permute-start | bytes 786440 | tf_op jit(solution)/shard_map/ppermute | solution.py:283
  62.3 13.4 %collective-permute-start.14 = (f16[2,128,1024]{2,1,0:T(8,128)(2,1)S(1)}, f16[2,128,1024]{2,1,0:T(8,128)(2,1)S(1)}, u32[]{:S(2)}, u32[]{:S(2)}) collective-permute-start(f16[2,128,1024]{2,1,0:T(8,128)(2,1)S(1)} %get-tuple-element.90), channel_id=1, source_target_pairs={{0,1},{1,0},{2,3},{3,2},{4,5},{5,4},{6,7},{7,6},{8,9},{9,8},{10,11... | collective-permute-start | bytes 1572872 | tf_op jit(solution)/shard_map/ppermute | solution.py:283
  69.7 8.8 %collective-permute-start.12 = (f16[2,128,1024]{2,1,0:T(8,128)(2,1)S(1)}, f16[2,128,1024]{2,1,0:T(8,128)(2,1)S(1)}, u32[]{:S(2)}, u32[]{:S(2)}) collective-permute-start(f16[2,128,1024]{2,1,0:T(8,128)(2,1)S(1)} %get-tuple-element.92), channel_id=1, source_target_pairs={{0,1},{1,0},{2,3},{3,2},{4,5},{5,4},{6,7},{7,6},{8,9},{9,8},{10,11... | collective-permute-start | bytes 1572872 | tf_op jit(solution)/shard_map/ppermute | solution.py:283
